TPU v7x, 512 devices: a whole 4x4x16 slice. The times are simulated.
512 devices in a mesh: db: 16 (over y_hi, x, core), pb: 32 (over y_lo, z).
Axes of the slice: x: 4, y: 4 (y_hi: 2, y_lo: 2; y = y_hi * 2 + y_lo), z: 16, core: 2. Of those that a mesh axis runs over, the one named last changes fastest.
Arguments:
- queries: bfloat16 [8192, 768], P(('db', 'pb')), may hold values from -14 to 14
- passage_codes: int32 [65536, 64], P(('db', 'pb')), may hold values from 0 to 255
- codebooks: bfloat16 [64, 12, 256], replicated, may hold values from -4 to 4
- positives: int32 [8192], P(('db', 'pb')), may hold values from 0 to 2047
- loss_weight: float32 [8192], P(('db', 'pb')), may hold values from -12 to 12
Outputs:
- query_loss: float32 [8192], P(('db', 'pb'))
- grad_queries: float32 [8192, 768], P(('db', 'pb'))
- grad_codebooks: float32 [64, 12, 256], replicated
All inputs are finite; a program needn't handle non-finite values.
Results may differ from a plain program's by a relative error of at most 0.0055.
Values may be sent and summed in bfloat16 or wider, within the bound.
No kernel may reach another device: no remote copies, remote signals or barrier semaphores. Data moves between devices by JAX's collectives and lax.ppermute only.
A program may use at most 64 MiB of HBM per device.

v0:
```python
import math

import jax
import jax.numpy as jnp
from jax import lax
from jax.sharding import PartitionSpec as P


def shifted(block, axis, distance):
    devices = range(lax.axis_size(axis))
    route = [((i - distance) % len(devices), i) for i in devices]
    return lax.ppermute(block, axis, route)


def code_table(code_rows, level_count):
    levels = jnp.arange(level_count, dtype=jnp.int32)
    return (levels[None, :, None] == code_rows[:, None, :]).astype(jnp.bfloat16)


def decode_cols(codebooks, passage_codes):
    book_count, sub_width, level_count = codebooks.shape
    passage_count = passage_codes.shape[0]
    code_sets = passage_codes.T.reshape(book_count // 4, 4, passage_count)
    book_sets = codebooks.reshape(book_count // 4, 4, sub_width, level_count)

    def decode_book_set(set_items):
        code_rows, book_rows = set_items
        table = code_table(code_rows, level_count)
        return jnp.einsum("mck,mkp->mcp", book_rows, table, preferred_element_type=jnp.float32)

    picked = lax.map(decode_book_set, (code_sets, book_sets))
    return picked.reshape(book_count * sub_width, passage_count).astype(jnp.bfloat16)


def book_part(passage_codes, grad_cols, codebooks):
    book_count, sub_width, level_count = codebooks.shape
    passage_count = passage_codes.shape[0]
    code_sets = passage_codes.T.reshape(book_count // 4, 4, passage_count)
    grad_sets = grad_cols.reshape(book_count // 4, 4, sub_width, passage_count)

    def book_book_set(set_items):
        code_rows, grad_rows = set_items
        table = code_table(code_rows, level_count)
        high_part = grad_rows.astype(jnp.bfloat16)
        low_part = (grad_rows - high_part.astype(jnp.float32)).astype(jnp.bfloat16)
        high_sum = jnp.einsum("mcp,mkp->mck", high_part, table, preferred_element_type=jnp.float32)
        low_sum = jnp.einsum("mcp,mkp->mck", low_part, table, preferred_element_type=jnp.float32)
        return high_sum + low_sum

    return lax.map(book_book_set, (code_sets, grad_sets)).reshape(
        book_count, sub_width, level_count
    )


def move_block(query_block):
    moved_block = shifted(query_block, "db", 1)
    return moved_block


def move_stats(running_max, running_sum):
    moved_stats = shifted((running_max, running_sum), "db", 1)
    return moved_stats


def move_grads(log_total, block_weight, block_target, block_chosen, block_grad):
    moved_grads = shifted(
        (log_total, block_weight, block_target, block_chosen, block_grad), "db", 1
    )
    return moved_grads


def fold_stats(running, scores):
    running_max, running_sum = running
    newest_max = jnp.maximum(running_max, jnp.max(scores, axis=1))
    running_sum = running_sum * jnp.exp(running_max - newest_max) + jnp.sum(
        jnp.exp(scores - newest_max[:, None]), axis=1
    )
    return (newest_max, running_sum)


def per_device(queries, passage_codes, codebooks, positives, loss_weight):
    query_rows, model_width = queries.shape
    passage_count = passage_codes.shape[0]
    logit_scale = 2.5 / math.sqrt(model_width)
    empty_max = jnp.full((query_rows,), -jnp.inf, jnp.float32)
    empty_rows = jnp.zeros((query_rows,), jnp.float32)
    empty_grad = jnp.zeros((query_rows, model_width), jnp.float32)
    decoded_cols = decode_cols(codebooks, passage_codes)
    spot_index = (
        lax.axis_index("db") * passage_count + jnp.arange(passage_count, dtype=jnp.int32)
    ).astype(jnp.float32)

    def stats_step(turn_index, state):
        query_block, running_max, running_sum = state
        scores = (
            jnp.dot(query_block, decoded_cols, preferred_element_type=jnp.float32) * logit_scale
        )
        newest_max, running_sum = fold_stats((running_max, running_sum), scores)
        query_block = move_block(query_block)
        newest_max, running_sum = move_stats(newest_max, running_sum)
        return (query_block, newest_max, running_sum)

    query_block, running_max, running_sum = lax.fori_loop(
        0, lax.axis_size("db"), stats_step, (queries, empty_max, empty_rows)
    )
    log_total = running_max + jnp.log(running_sum)

    def grad_step(turn_index, state):
        (
            query_block,
            block_total,
            block_weight,
            block_target,
            block_chosen,
            block_grad,
            passage_grad,
        ) = state
        scores = (
            jnp.dot(query_block, decoded_cols, preferred_element_type=jnp.float32) * logit_scale
        )
        is_positive = block_target[:, None] == spot_index[None, :]
        block_chosen = block_chosen + jnp.sum(jnp.where(is_positive, scores, 0.0), axis=1)
        coefficient = (
            block_weight[:, None]
            * (jnp.exp(scores - block_total[:, None]) - is_positive.astype(jnp.float32))
            * logit_scale
        ).astype(jnp.bfloat16)
        block_grad = block_grad + jnp.einsum(
            "qp,dp->qd", coefficient, decoded_cols, preferred_element_type=jnp.float32
        )
        passage_grad = passage_grad + jnp.einsum(
            "qd,qp->dp", query_block, coefficient, preferred_element_type=jnp.float32
        )
        query_block = move_block(query_block)
        block_total, block_weight, block_target, block_chosen, block_grad = move_grads(
            block_total, block_weight, block_target, block_chosen, block_grad
        )
        return (
            query_block,
            block_total,
            block_weight,
            block_target,
            block_chosen,
            block_grad,
            passage_grad,
        )

    start_state = (
        queries,
        log_total,
        loss_weight,
        positives.astype(jnp.float32),
        empty_rows,
        empty_grad,
        jnp.zeros((model_width, passage_count), jnp.float32),
    )
    final_state = lax.fori_loop(0, lax.axis_size("db"), grad_step, start_state)
    chosen = final_state[4]
    grad_queries = final_state[5]
    book_grad = book_part(passage_codes, final_state[6], codebooks)
    query_loss = loss_weight * (log_total - chosen)
    book_total = lax.psum(book_grad, ("db", "pb"))
    return (query_loss, grad_queries, book_total)


def solution(mesh):
    return jax.shard_map(
        per_device,
        mesh=mesh,
        in_specs=(
            P(("db", "pb"), None),
            P(("db", "pb"), None),
            P(),
            P(("db", "pb")),
            P(("db", "pb")),
        ),
        out_specs=(P(("db", "pb")), P(("db", "pb"), None), P()),
        check_vma=False,
    )
```

profile of v0, /device:TPU:1, one launch (start us, length us, event | category | flops | bytes accessed | tf_op | source)
XLA Modules:
  0.0 1142.7 jit_solution(6119165569938202182)
XLA Ops:
  9.2 14.4 %while.57 = (s32[]{:T(128)}, bf16[16,4,12,128]{3,2,1,0:T(8,128)(2,1)S(1)}, bf16[16,4,12,256]{3,2,1,0:T(8,128)(2,1)S(1)}, s32[16,4,128]{2,1,0:T(4,128)}, s32[]{:T(128)}) while((s32[]{:T(128)}, bf16[16,4,12,128]{3,2,1,0:T(8,128)(2,1)S(1)}, bf16[16,4,12,256]{3,2,1,0:T(8,128)(2,1)S(1)}, s32[16,4,128]{2,1,0:T(4,128)}, s32[]{:T(128)}) %tuple.90), condition=%wide.region_1.2_spmd, body=%wide.region_0.1_spmd.sunk | while | flops 3276802 | bytes 72769 | solution.py:31
  23.6 206.1 %while.58 = (s32[]{:T(128)}, bf16[16,768]{1,0:T(8,128)(2,1)S(1)}, f32[16]{0:T(128)S(1)}, f32[16]{0:T(128)S(1)}, bf16[768,128]{1,0:T(8,128)(2,1)S(1)}, /*index=5*/s32[]{:T(128)}) while((s32[]{:T(128)}, bf16[16,768]{1,0:T(8,128)(2,1)S(1)}, f32[16]{0:T(128)S(1)}, f32[16]{0:T(128)S(1)}, bf16[768,128]{1,0:T(8,128)(2,1)S(1)}, ...), condition=%wide.region_5.6_spmd, body=%wide.region_2.5_spmd.sunk | while | flops 3153954 | bytes 386557 | solution.py:103
  23.6 4.5 collective-permute-start
  30.5 3.5 collective-permute-start.2
  44.5 3.5 collective-permute-done.1
  57.0 3.9 collective-permute-done.1
  67.3 4.0 collective-permute-start.2
  80.1 4.0 collective-permute-start.2
  93.0 4.0 collective-permute-start.2
  105.8 4.0 collective-permute-start.2
  118.6 4.0 collective-permute-start.2
  131.4 4.0 collective-permute-start.2
  144.2 4.0 collective-permute-start.2
  157.1 4.0 collective-permute-start.2
  169.9 4.0 collective-permute-start.2
  182.7 4.0 collective-permute-start.2
  195.5 4.0 collective-permute-start.2
  208.4 4.0 collective-permute-start.2
  221.2 4.0 collective-permute-start.2
  231.5 404.3 %while.60 = (s32[]{:T(128)}, bf16[16,768]{1,0:T(8,128)(2,1)S(1)}, f32[16]{0:T(128)S(1)}, f32[16]{0:T(128)S(1)}, f32[16]{0:T(128)S(1)}, /*index=5*/f32[16]{0:T(12...) while((s32[]{:T(128)}, bf16[16,768]{1,0:T(8,128)(2,1)S(1)}, ...), condition=%wide.region_8.9_spmd.clone, body=%wide.region_6.8_spmd.clone.sunk | while | flops 9683203 | bytes 1700275 | solution.py:157
  235.4 4.0 collective-permute-start.4
  239.9 3.3 collective-permute-start.8
  243.3 4.2 collective-permute-start.7
  248.3 4.0 collective-permute-start.5
  252.3 4.4 collective-permute-done.5
  260.7 4.0 collective-permute-start.4
  269.5 4.1 collective-permute-done.7
  275.5 6.6 collective-permute-done.5
  284.0 3.1 collective-permute-start.3
  287.1 4.2 collective-permute-start.4
  300.8 6.6 collective-permute-done.5
  309.3 3.1 collective-permute-start.3
  312.4 4.2 collective-permute-start.4
  326.0 6.6 collective-permute-done.5
  334.5 3.1 collective-permute-start.3
  337.6 4.2 collective-permute-start.4
  351.3 6.6 collective-permute-done.5
  359.8 3.1 collective-permute-start.3
  362.9 4.2 collective-permute-start.4
  376.6 6.6 collective-permute-done.5
  385.1 3.1 collective-permute-start.3
  388.2 4.2 collective-permute-start.4
  401.8 6.6 collective-permute-done.5
  410.3 3.1 collective-permute-start.3
  413.5 4.2 collective-permute-start.4
  427.1 6.6 collective-permute-done.5
  438.7 4.2 collective-permute-start.4
  452.4 6.6 collective-permute-done.5
  464.0 4.2 collective-permute-start.4
  477.6 6.6 collective-permute-done.5
  489.3 4.2 collective-permute-start.4
  502.9 6.6 collective-permute-done.5
  514.5 4.2 collective-permute-start.4
  528.2 6.6 collective-permute-done.5
  539.8 4.2 collective-permute-start.4
  553.4 6.6 collective-permute-done.5
  565.1 4.2 collective-permute-start.4
  578.7 6.6 collective-permute-done.5
  590.3 4.2 collective-permute-start.4
  604.0 6.6 collective-permute-done.5
  615.6 4.2 collective-permute-start.4
  629.2 6.6 collective-permute-done.5
  636.0 17.6 %while.59 = (s32[]{:T(128)}, f32[16,4,12,256]{3,2,1,0:T(8,128)S(1)}, f32[16,4,12,128]{3,2,1,0:T(8,128)S(1)}, s32[16,4,128]{2,1,0:T(4,128)}, s32[]{:T(128)}) while((s32[]{:T(128)}, f32[16,4,12,256]{3,2,1,0:T(8,128)S(1)}, f32[16,4,12,128]{3,2,1,0:T(8,128)S(1)}, s32[16,4,128]{2,1,0:T(4,128)}, s32[]{:T(128)}) %tuple.91), condition=%wide.region_10.11_spmd, body=%wide.region_9.10_spmd.sunk | while | flops 6590466 | bytes 238661 | solution.py:50
  656.1 477.0 %all-reduce.2.cloned.1.call-done = f32[64,12,256]{2,0,1:T(8,128)} async-done(((f32[64,12,256]{2,0,1:T(8,128)}), f32[64,12,256]{2,0,1:T(8,128)}) %all-reduce.2.cloned.1.call-update) | async-done | bytes 786448 | tf_op jit(solution)/shard_map/psum | solution.py:162
  (582 shorter events, 377.4 us)
Async XLA Ops:
  7.2 1126.0 %all-reduce.2.cloned.1.call-start = ((), (), s32[]{:S(2)}) async-start(), calls=%async_computation | async-start | bytes 1572864 | tf_op jit(solution)/shard_map/psum | solution.py:162
  23.6 13.7 %collective-permute-start = (bf16[16,768]{1,0:T(8,128)(2,1)S(1)}, bf16[16,768]{1,0:T(8,128)(2,1)S(1)}, u32[]{:S(2)}, u32[]{:S(2)}) collective-permute-start(bf16[16,768]{1,0:T(8,128)(2,1)S(1)} %copy.28), channel_id=1, source_target_pairs={{480,0},{0,32},{32,64},{64,96},{96,128},{128,160},{160,192},{192,2... | collective-permute-start | bytes 73736 | tf_op jit(solution)/shard_map/while/body/eval_jaxpr/ppermute | solution.py:12
  231.5 20.8 %collective-permute-start.6 = (f32[16]{0:T(128)S(1)}, f32[16]{0:T(128)S(1)}, u32[]{:S(2)}, u32[]{:S(2)}) collective-permute-start(f32[16]{0:T(128)S(1)} %copy.47), channel_id=1, source_target_pairs={{480,0},{0,32},{32,64},{64,96},{96,128},{128,160},{160,192},{192,2... | collective-permute-start | bytes 200 | tf_op jit(solution)/shard_map/while/body/eval_jaxpr/ppermute | solution.py:12
  233.5 23.3 %collective-permute-start.3 = (bf16[16,768]{1,0:T(8,128)(2,1)S(1)}, bf16[16,768]{1,0:T(8,128)(2,1)S(1)}, u32[]{:S(2)}, u32[]{:S(2)}) collective-permute-start(bf16[16,768]{1,0:T(8,128)(2,1)S(1)} %copy.44), channel_id=1, source_target_pairs={{480,0},{0,32},{32,64},{64,96},{96,128},{128,160},{160,192},{192,2... | collective-permute-start | bytes 73736 | tf_op jit(solution)/shard_map/while/body/eval_jaxpr/ppermute | solution.py:12
  235.4 16.9 %collective-permute-start.4 = (f32[16]{0:T(128)S(1)}, f32[16]{0:T(128)S(1)}, u32[]{:S(2)}, u32[]{:S(2)}) collective-permute-start(f32[16]{0:T(128)S(1)} %copy.45), channel_id=1, source_target_pairs={{480,0},{0,32},{32,64},{64,96},{96,128},{128,160},{160,192},{192,2... | collective-permute-start | bytes 200 | tf_op jit(solution)/shard_map/while/body/eval_jaxpr/ppermute | solution.py:12
  239.9 16.8 %collective-permute-start.8 = (f32[16,768]{1,0:T(8,128)S(1)}, f32[16,768]{1,0:T(8,128)S(1)}, u32[]{:S(2)}, u32[]{:S(2)}) collective-permute-start(f32[16,768]{1,0:T(8,128)S(1)} %convolution_add_fusion.3), channel_id=1, source_target_pairs={{480,0},{0,32},{32,64},{64,96},{96,128},{128,160},{160,192},{192,2... | collective-permute-start | bytes 147464 | tf_op jit(solution)/shard_map/while/body/eval_jaxpr/ppermute | solution.py:12
  256.8 18.7 %collective-permute-start.6 = (f32[16]{0:T(128)S(1)}, f32[16]{0:T(128)S(1)}, u32[]{:S(2)}, u32[]{:S(2)}) collective-permute-start(f32[16]{0:T(128)S(1)} %copy.47), channel_id=1, source_target_pairs={{480,0},{0,32},{32,64},{64,96},{96,128},{128,160},{160,192},{192,2... | collective-permute-start | bytes 200 | tf_op jit(solution)/shard_map/while/body/eval_jaxpr/ppermute | solution.py:12
  258.7 23.3 %collective-permute-start.3 = (bf16[16,768]{1,0:T(8,128)(2,1)S(1)}, bf16[16,768]{1,0:T(8,128)(2,1)S(1)}, u32[]{:S(2)}, u32[]{:S(2)}) collective-permute-start(bf16[16,768]{1,0:T(8,128)(2,1)S(1)} %copy.44), channel_id=1, source_target_pairs={{480,0},{0,32},{32,64},{64,96},{96,128},{128,160},{160,192},{192,2... | collective-permute-start | bytes 73736 | tf_op jit(solution)/shard_map/while/body/eval_jaxpr/ppermute | solution.py:12
  260.7 14.8 %collective-permute-start.4 = (f32[16]{0:T(128)S(1)}, f32[16]{0:T(128)S(1)}, u32[]{:S(2)}, u32[]{:S(2)}) collective-permute-start(f32[16]{0:T(128)S(1)} %copy.45), channel_id=1, source_target_pairs={{480,0},{0,32},{32,64},{64,96},{96,128},{128,160},{160,192},{192,2... | collective-permute-start | bytes 200 | tf_op jit(solution)/shard_map/while/body/eval_jaxpr/ppermute | solution.py:12
  265.2 16.8 %collective-permute-start.8 = (f32[16,768]{1,0:T(8,128)S(1)}, f32[16,768]{1,0:T(8,128)S(1)}, u32[]{:S(2)}, u32[]{:S(2)}) collective-permute-start(f32[16,768]{1,0:T(8,128)S(1)} %convolution_add_fusion.3), channel_id=1, source_target_pairs={{480,0},{0,32},{32,64},{64,96},{96,128},{128,160},{160,192},{192,2... | collective-permute-start | bytes 147464 | tf_op jit(solution)/shard_map/while/body/eval_jaxpr/ppermute | solution.py:12
  282.1 18.7 %collective-permute-start.6 = (f32[16]{0:T(128)S(1)}, f32[16]{0:T(128)S(1)}, u32[]{:S(2)}, u32[]{:S(2)}) collective-permute-start(f32[16]{0:T(128)S(1)} %copy.47), channel_id=1, source_target_pairs={{480,0},{0,32},{32,64},{64,96},{96,128},{128,160},{160,192},{192,2... | collective-permute-start | bytes 200 | tf_op jit(solution)/shard_map/while/body/eval_jaxpr/ppermute | solution.py:12
  284.0 23.3 %collective-permute-start.3 = (bf16[16,768]{1,0:T(8,128)(2,1)S(1)}, bf16[16,768]{1,0:T(8,128)(2,1)S(1)}, u32[]{:S(2)}, u32[]{:S(2)}) collective-permute-start(bf16[16,768]{1,0:T(8,128)(2,1)S(1)} %copy.44), channel_id=1, source_target_pairs={{480,0},{0,32},{32,64},{64,96},{96,128},{128,160},{160,192},{192,2... | collective-permute-start | bytes 73736 | tf_op jit(solution)/shard_map/while/body/eval_jaxpr/ppermute | solution.py:12
  287.1 13.6 %collective-permute-start.4 = (f32[16]{0:T(128)S(1)}, f32[16]{0:T(128)S(1)}, u32[]{:S(2)}, u32[]{:S(2)}) collective-permute-start(f32[16]{0:T(128)S(1)} %copy.45), channel_id=1, source_target_pairs={{480,0},{0,32},{32,64},{64,96},{96,128},{128,160},{160,192},{192,2... | collective-permute-start | bytes 200 | tf_op jit(solution)/shard_map/while/body/eval_jaxpr/ppermute | solution.py:12
  291.8 15.5 %collective-permute-start.8 = (f32[16,768]{1,0:T(8,128)S(1)}, f32[16,768]{1,0:T(8,128)S(1)}, u32[]{:S(2)}, u32[]{:S(2)}) collective-permute-start(f32[16,768]{1,0:T(8,128)S(1)} %convolution_add_fusion.3), channel_id=1, source_target_pairs={{480,0},{0,32},{32,64},{64,96},{96,128},{128,160},{160,192},{192,2... | collective-permute-start | bytes 147464 | tf_op jit(solution)/shard_map/while/body/eval_jaxpr/ppermute | solution.py:12
  307.3 18.7 %collective-permute-start.6 = (f32[16]{0:T(128)S(1)}, f32[16]{0:T(128)S(1)}, u32[]{:S(2)}, u32[]{:S(2)}) collective-permute-start(f32[16]{0:T(128)S(1)} %copy.47), channel_id=1, source_target_pairs={{480,0},{0,32},{32,64},{64,96},{96,128},{128,160},{160,192},{192,2... | collective-permute-start | bytes 200 | tf_op jit(solution)/shard_map/while/body/eval_jaxpr/ppermute | solution.py:12
  309.3 23.3 %collective-permute-start.3 = (bf16[16,768]{1,0:T(8,128)(2,1)S(1)}, bf16[16,768]{1,0:T(8,128)(2,1)S(1)}, u32[]{:S(2)}, u32[]{:S(2)}) collective-permute-start(bf16[16,768]{1,0:T(8,128)(2,1)S(1)} %copy.44), channel_id=1, source_target_pairs={{480,0},{0,32},{32,64},{64,96},{96,128},{128,160},{160,192},{192,2... | collective-permute-start | bytes 73736 | tf_op jit(solution)/shard_map/while/body/eval_jaxpr/ppermute | solution.py:12
  312.4 13.6 %collective-permute-start.4 = (f32[16]{0:T(128)S(1)}, f32[16]{0:T(128)S(1)}, u32[]{:S(2)}, u32[]{:S(2)}) collective-permute-start(f32[16]{0:T(128)S(1)} %copy.45), channel_id=1, source_target_pairs={{480,0},{0,32},{32,64},{64,96},{96,128},{128,160},{160,192},{192,2... | collective-permute-start | bytes 200 | tf_op jit(solution)/shard_map/while/body/eval_jaxpr/ppermute | solution.py:12
  317.1 15.5 %collective-permute-start.8 = (f32[16,768]{1,0:T(8,128)S(1)}, f32[16,768]{1,0:T(8,128)S(1)}, u32[]{:S(2)}, u32[]{:S(2)}) collective-permute-start(f32[16,768]{1,0:T(8,128)S(1)} %convolution_add_fusion.3), channel_id=1, source_target_pairs={{480,0},{0,32},{32,64},{64,96},{96,128},{128,160},{160,192},{192,2... | collective-permute-start | bytes 147464 | tf_op jit(solution)/shard_map/while/body/eval_jaxpr/ppermute | solution.py:12
  332.6 18.7 %collective-permute-start.6 = (f32[16]{0:T(128)S(1)}, f32[16]{0:T(128)S(1)}, u32[]{:S(2)}, u32[]{:S(2)}) collective-permute-start(f32[16]{0:T(128)S(1)} %copy.47), channel_id=1, source_target_pairs={{480,0},{0,32},{32,64},{64,96},{96,128},{128,160},{160,192},{192,2... | collective-permute-start | bytes 200 | tf_op jit(solution)/shard_map/while/body/eval_jaxpr/ppermute | solution.py:12
  334.5 23.3 %collective-permute-start.3 = (bf16[16,768]{1,0:T(8,128)(2,1)S(1)}, bf16[16,768]{1,0:T(8,128)(2,1)S(1)}, u32[]{:S(2)}, u32[]{:S(2)}) collective-permute-start(bf16[16,768]{1,0:T(8,128)(2,1)S(1)} %copy.44), channel_id=1, source_target_pairs={{480,0},{0,32},{32,64},{64,96},{96,128},{128,160},{160,192},{192,2... | collective-permute-start | bytes 73736 | tf_op jit(solution)/shard_map/while/body/eval_jaxpr/ppermute | solution.py:12
  337.6 13.6 %collective-permute-start.4 = (f32[16]{0:T(128)S(1)}, f32[16]{0:T(128)S(1)}, u32[]{:S(2)}, u32[]{:S(2)}) collective-permute-start(f32[16]{0:T(128)S(1)} %copy.45), channel_id=1, source_target_pairs={{480,0},{0,32},{32,64},{64,96},{96,128},{128,160},{160,192},{192,2... | collective-permute-start | bytes 200 | tf_op jit(solution)/shard_map/while/body/eval_jaxpr/ppermute | solution.py:12
  342.3 15.5 %collective-permute-start.8 = (f32[16,768]{1,0:T(8,128)S(1)}, f32[16,768]{1,0:T(8,128)S(1)}, u32[]{:S(2)}, u32[]{:S(2)}) collective-permute-start(f32[16,768]{1,0:T(8,128)S(1)} %convolution_add_fusion.3), channel_id=1, source_target_pairs={{480,0},{0,32},{32,64},{64,96},{96,128},{128,160},{160,192},{192,2... | collective-permute-start | bytes 147464 | tf_op jit(solution)/shard_map/while/body/eval_jaxpr/ppermute | solution.py:12
  357.9 18.7 %collective-permute-start.6 = (f32[16]{0:T(128)S(1)}, f32[16]{0:T(128)S(1)}, u32[]{:S(2)}, u32[]{:S(2)}) collective-permute-start(f32[16]{0:T(128)S(1)} %copy.47), channel_id=1, source_target_pairs={{480,0},{0,32},{32,64},{64,96},{96,128},{128,160},{160,192},{192,2... | collective-permute-start | bytes 200 | tf_op jit(solution)/shard_map/while/body/eval_jaxpr/ppermute | solution.py:12
  359.8 23.3 %collective-permute-start.3 = (bf16[16,768]{1,0:T(8,128)(2,1)S(1)}, bf16[16,768]{1,0:T(8,128)(2,1)S(1)}, u32[]{:S(2)}, u32[]{:S(2)}) collective-permute-start(bf16[16,768]{1,0:T(8,128)(2,1)S(1)} %copy.44), channel_id=1, source_target_pairs={{480,0},{0,32},{32,64},{64,96},{96,128},{128,160},{160,192},{192,2... | collective-permute-start | bytes 73736 | tf_op jit(solution)/shard_map/while/body/eval_jaxpr/ppermute | solution.py:12
  362.9 13.6 %collective-permute-start.4 = (f32[16]{0:T(128)S(1)}, f32[16]{0:T(128)S(1)}, u32[]{:S(2)}, u32[]{:S(2)}) collective-permute-start(f32[16]{0:T(128)S(1)} %copy.45), channel_id=1, source_target_pairs={{480,0},{0,32},{32,64},{64,96},{96,128},{128,160},{160,192},{192,2... | collective-permute-start | bytes 200 | tf_op jit(solution)/shard_map/while/body/eval_jaxpr/ppermute | solution.py:12
  367.6 15.5 %collective-permute-start.8 = (f32[16,768]{1,0:T(8,128)S(1)}, f32[16,768]{1,0:T(8,128)S(1)}, u32[]{:S(2)}, u32[]{:S(2)}) collective-permute-start(f32[16,768]{1,0:T(8,128)S(1)} %convolution_add_fusion.3), channel_id=1, source_target_pairs={{480,0},{0,32},{32,64},{64,96},{96,128},{128,160},{160,192},{192,2... | collective-permute-start | bytes 147464 | tf_op jit(solution)/shard_map/while/body/eval_jaxpr/ppermute | solution.py:12
  383.1 18.7 %collective-permute-start.6 = (f32[16]{0:T(128)S(1)}, f32[16]{0:T(128)S(1)}, u32[]{:S(2)}, u32[]{:S(2)}) collective-permute-start(f32[16]{0:T(128)S(1)} %copy.47), channel_id=1, source_target_pairs={{480,0},{0,32},{32,64},{64,96},{96,128},{128,160},{160,192},{192,2... | collective-permute-start | bytes 200 | tf_op jit(solution)/shard_map/while/body/eval_jaxpr/ppermute | solution.py:12
  385.1 23.3 %collective-permute-start.3 = (bf16[16,768]{1,0:T(8,128)(2,1)S(1)}, bf16[16,768]{1,0:T(8,128)(2,1)S(1)}, u32[]{:S(2)}, u32[]{:S(2)}) collective-permute-start(bf16[16,768]{1,0:T(8,128)(2,1)S(1)} %copy.44), channel_id=1, source_target_pairs={{480,0},{0,32},{32,64},{64,96},{96,128},{128,160},{160,192},{192,2... | collective-permute-start | bytes 73736 | tf_op jit(solution)/shard_map/while/body/eval_jaxpr/ppermute | solution.py:12
  388.2 13.6 %collective-permute-start.4 = (f32[16]{0:T(128)S(1)}, f32[16]{0:T(128)S(1)}, u32[]{:S(2)}, u32[]{:S(2)}) collective-permute-start(f32[16]{0:T(128)S(1)} %copy.45), channel_id=1, source_target_pairs={{480,0},{0,32},{32,64},{64,96},{96,128},{128,160},{160,192},{192,2... | collective-permute-start | bytes 200 | tf_op jit(solution)/shard_map/while/body/eval_jaxpr/ppermute | solution.py:12
  392.9 15.5 %collective-permute-start.8 = (f32[16,768]{1,0:T(8,128)S(1)}, f32[16,768]{1,0:T(8,128)S(1)}, u32[]{:S(2)}, u32[]{:S(2)}) collective-permute-start(f32[16,768]{1,0:T(8,128)S(1)} %convolution_add_fusion.3), channel_id=1, source_target_pairs={{480,0},{0,32},{32,64},{64,96},{96,128},{128,160},{160,192},{192,2... | collective-permute-start | bytes 147464 | tf_op jit(solution)/shard_map/while/body/eval_jaxpr/ppermute | solution.py:12
  408.4 18.7 %collective-permute-start.6 = (f32[16]{0:T(128)S(1)}, f32[16]{0:T(128)S(1)}, u32[]{:S(2)}, u32[]{:S(2)}) collective-permute-start(f32[16]{0:T(128)S(1)} %copy.47), channel_id=1, source_target_pairs={{480,0},{0,32},{32,64},{64,96},{96,128},{128,160},{160,192},{192,2... | collective-permute-start | bytes 200 | tf_op jit(solution)/shard_map/while/body/eval_jaxpr/ppermute | solution.py:12
  410.3 23.3 %collective-permute-start.3 = (bf16[16,768]{1,0:T(8,128)(2,1)S(1)}, bf16[16,768]{1,0:T(8,128)(2,1)S(1)}, u32[]{:S(2)}, u32[]{:S(2)}) collective-permute-start(bf16[16,768]{1,0:T(8,128)(2,1)S(1)} %copy.44), channel_id=1, source_target_pairs={{480,0},{0,32},{32,64},{64,96},{96,128},{128,160},{160,192},{192,2... | collective-permute-start | bytes 73736 | tf_op jit(solution)/shard_map/while/body/eval_jaxpr/ppermute | solution.py:12
  413.5 13.6 %collective-permute-start.4 = (f32[16]{0:T(128)S(1)}, f32[16]{0:T(128)S(1)}, u32[]{:S(2)}, u32[]{:S(2)}) collective-permute-start(f32[16]{0:T(128)S(1)} %copy.45), channel_id=1, source_target_pairs={{480,0},{0,32},{32,64},{64,96},{96,128},{128,160},{160,192},{192,2... | collective-permute-start | bytes 200 | tf_op jit(solution)/shard_map/while/body/eval_jaxpr/ppermute | solution.py:12
  418.1 15.5 %collective-permute-start.8 = (f32[16,768]{1,0:T(8,128)S(1)}, f32[16,768]{1,0:T(8,128)S(1)}, u32[]{:S(2)}, u32[]{:S(2)}) collective-permute-start(f32[16,768]{1,0:T(8,128)S(1)} %convolution_add_fusion.3), channel_id=1, source_target_pairs={{480,0},{0,32},{32,64},{64,96},{96,128},{128,160},{160,192},{192,2... | collective-permute-start | bytes 147464 | tf_op jit(solution)/shard_map/while/body/eval_jaxpr/ppermute | solution.py:12
  433.7 18.7 %collective-permute-start.6 = (f32[16]{0:T(128)S(1)}, f32[16]{0:T(128)S(1)}, u32[]{:S(2)}, u32[]{:S(2)}) collective-permute-start(f32[16]{0:T(128)S(1)} %copy.47), channel_id=1, source_target_pairs={{480,0},{0,32},{32,64},{64,96},{96,128},{128,160},{160,192},{192,2... | collective-permute-start | bytes 200 | tf_op jit(solution)/shard_map/while/body/eval_jaxpr/ppermute | solution.py:12
  435.6 23.3 %collective-permute-start.3 = (bf16[16,768]{1,0:T(8,128)(2,1)S(1)}, bf16[16,768]{1,0:T(8,128)(2,1)S(1)}, u32[]{:S(2)}, u32[]{:S(2)}) collective-permute-start(bf16[16,768]{1,0:T(8,128)(2,1)S(1)} %copy.44), channel_id=1, source_target_pairs={{480,0},{0,32},{32,64},{64,96},{96,128},{128,160},{160,192},{192,2... | collective-permute-start | bytes 73736 | tf_op jit(solution)/shard_map/while/body/eval_jaxpr/ppermute | solution.py:12
  438.7 13.6 %collective-permute-start.4 = (f32[16]{0:T(128)S(1)}, f32[16]{0:T(128)S(1)}, u32[]{:S(2)}, u32[]{:S(2)}) collective-permute-start(f32[16]{0:T(128)S(1)} %copy.45), channel_id=1, source_target_pairs={{480,0},{0,32},{32,64},{64,96},{96,128},{128,160},{160,192},{192,2... | collective-permute-start | bytes 200 | tf_op jit(solution)/shard_map/while/body/eval_jaxpr/ppermute | solution.py:12
  443.4 15.5 %collective-permute-start.8 = (f32[16,768]{1,0:T(8,128)S(1)}, f32[16,768]{1,0:T(8,128)S(1)}, u32[]{:S(2)}, u32[]{:S(2)}) collective-permute-start(f32[16,768]{1,0:T(8,128)S(1)} %convolution_add_fusion.3), channel_id=1, source_target_pairs={{480,0},{0,32},{32,64},{64,96},{96,128},{128,160},{160,192},{192,2... | collective-permute-start | bytes 147464 | tf_op jit(solution)/shard_map/while/body/eval_jaxpr/ppermute | solution.py:12
  458.9 18.7 %collective-permute-start.6 = (f32[16]{0:T(128)S(1)}, f32[16]{0:T(128)S(1)}, u32[]{:S(2)}, u32[]{:S(2)}) collective-permute-start(f32[16]{0:T(128)S(1)} %copy.47), channel_id=1, source_target_pairs={{480,0},{0,32},{32,64},{64,96},{96,128},{128,160},{160,192},{192,2... | collective-permute-start | bytes 200 | tf_op jit(solution)/shard_map/while/body/eval_jaxpr/ppermute | solution.py:12
  460.9 23.3 %collective-permute-start.3 = (bf16[16,768]{1,0:T(8,128)(2,1)S(1)}, bf16[16,768]{1,0:T(8,128)(2,1)S(1)}, u32[]{:S(2)}, u32[]{:S(2)}) collective-permute-start(bf16[16,768]{1,0:T(8,128)(2,1)S(1)} %copy.44), channel_id=1, source_target_pairs={{480,0},{0,32},{32,64},{64,96},{96,128},{128,160},{160,192},{192,2... | collective-permute-start | bytes 73736 | tf_op jit(solution)/shard_map/while/body/eval_jaxpr/ppermute | solution.py:12
  468.7 15.5 %collective-permute-start.8 = (f32[16,768]{1,0:T(8,128)S(1)}, f32[16,768]{1,0:T(8,128)S(1)}, u32[]{:S(2)}, u32[]{:S(2)}) collective-permute-start(f32[16,768]{1,0:T(8,128)S(1)} %convolution_add_fusion.3), channel_id=1, source_target_pairs={{480,0},{0,32},{32,64},{64,96},{96,128},{128,160},{160,192},{192,2... | collective-permute-start | bytes 147464 | tf_op jit(solution)/shard_map/while/body/eval_jaxpr/ppermute | solution.py:12
  484.2 18.7 %collective-permute-start.6 = (f32[16]{0:T(128)S(1)}, f32[16]{0:T(128)S(1)}, u32[]{:S(2)}, u32[]{:S(2)}) collective-permute-start(f32[16]{0:T(128)S(1)} %copy.47), channel_id=1, source_target_pairs={{480,0},{0,32},{32,64},{64,96},{96,128},{128,160},{160,192},{192,2... | collective-permute-start | bytes 200 | tf_op jit(solution)/shard_map/while/body/eval_jaxpr/ppermute | solution.py:12
  486.1 23.3 %collective-permute-start.3 = (bf16[16,768]{1,0:T(8,128)(2,1)S(1)}, bf16[16,768]{1,0:T(8,128)(2,1)S(1)}, u32[]{:S(2)}, u32[]{:S(2)}) collective-permute-start(bf16[16,768]{1,0:T(8,128)(2,1)S(1)} %copy.44), channel_id=1, source_target_pairs={{480,0},{0,32},{32,64},{64,96},{96,128},{128,160},{160,192},{192,2... | collective-permute-start | bytes 73736 | tf_op jit(solution)/shard_map/while/body/eval_jaxpr/ppermute | solution.py:12
  489.3 13.6 %collective-permute-start.4 = (f32[16]{0:T(128)S(1)}, f32[16]{0:T(128)S(1)}, u32[]{:S(2)}, u32[]{:S(2)}) collective-permute-start(f32[16]{0:T(128)S(1)} %copy.45), channel_id=1, source_target_pairs={{480,0},{0,32},{32,64},{64,96},{96,128},{128,160},{160,192},{192,2... | collective-permute-start | bytes 200 | tf_op jit(solution)/shard_map/while/body/eval_jaxpr/ppermute | solution.py:12
  493.9 15.5 %collective-permute-start.8 = (f32[16,768]{1,0:T(8,128)S(1)}, f32[16,768]{1,0:T(8,128)S(1)}, u32[]{:S(2)}, u32[]{:S(2)}) collective-permute-start(f32[16,768]{1,0:T(8,128)S(1)} %convolution_add_fusion.3), channel_id=1, source_target_pairs={{480,0},{0,32},{32,64},{64,96},{96,128},{128,160},{160,192},{192,2... | collective-permute-start | bytes 147464 | tf_op jit(solution)/shard_map/while/body/eval_jaxpr/ppermute | solution.py:12
  509.5 18.7 %collective-permute-start.6 = (f32[16]{0:T(128)S(1)}, f32[16]{0:T(128)S(1)}, u32[]{:S(2)}, u32[]{:S(2)}) collective-permute-start(f32[16]{0:T(128)S(1)} %copy.47), channel_id=1, source_target_pairs={{480,0},{0,32},{32,64},{64,96},{96,128},{128,160},{160,192},{192,2... | collective-permute-start | bytes 200 | tf_op jit(solution)/shard_map/while/body/eval_jaxpr/ppermute | solution.py:12
  511.4 23.3 %collective-permute-start.3 = (bf16[16,768]{1,0:T(8,128)(2,1)S(1)}, bf16[16,768]{1,0:T(8,128)(2,1)S(1)}, u32[]{:S(2)}, u32[]{:S(2)}) collective-permute-start(bf16[16,768]{1,0:T(8,128)(2,1)S(1)} %copy.44), channel_id=1, source_target_pairs={{480,0},{0,32},{32,64},{64,96},{96,128},{128,160},{160,192},{192,2... | collective-permute-start | bytes 73736 | tf_op jit(solution)/shard_map/while/body/eval_jaxpr/ppermute | solution.py:12
  514.5 13.6 %collective-permute-start.4 = (f32[16]{0:T(128)S(1)}, f32[16]{0:T(128)S(1)}, u32[]{:S(2)}, u32[]{:S(2)}) collective-permute-start(f32[16]{0:T(128)S(1)} %copy.45), channel_id=1, source_target_pairs={{480,0},{0,32},{32,64},{64,96},{96,128},{128,160},{160,192},{192,2... | collective-permute-start | bytes 200 | tf_op jit(solution)/shard_map/while/body/eval_jaxpr/ppermute | solution.py:12
  519.2 15.5 %collective-permute-start.8 = (f32[16,768]{1,0:T(8,128)S(1)}, f32[16,768]{1,0:T(8,128)S(1)}, u32[]{:S(2)}, u32[]{:S(2)}) collective-permute-start(f32[16,768]{1,0:T(8,128)S(1)} %convolution_add_fusion.3), channel_id=1, source_target_pairs={{480,0},{0,32},{32,64},{64,96},{96,128},{128,160},{160,192},{192,2... | collective-permute-start | bytes 147464 | tf_op jit(solution)/shard_map/while/body/eval_jaxpr/ppermute | solution.py:12
  534.7 18.7 %collective-permute-start.6 = (f32[16]{0:T(128)S(1)}, f32[16]{0:T(128)S(1)}, u32[]{:S(2)}, u32[]{:S(2)}) collective-permute-start(f32[16]{0:T(128)S(1)} %copy.47), channel_id=1, source_target_pairs={{480,0},{0,32},{32,64},{64,96},{96,128},{128,160},{160,192},{192,2... | collective-permute-start | bytes 200 | tf_op jit(solution)/shard_map/while/body/eval_jaxpr/ppermute | solution.py:12
  536.7 23.3 %collective-permute-start.3 = (bf16[16,768]{1,0:T(8,128)(2,1)S(1)}, bf16[16,768]{1,0:T(8,128)(2,1)S(1)}, u32[]{:S(2)}, u32[]{:S(2)}) collective-permute-start(bf16[16,768]{1,0:T(8,128)(2,1)S(1)} %copy.44), channel_id=1, source_target_pairs={{480,0},{0,32},{32,64},{64,96},{96,128},{128,160},{160,192},{192,2... | collective-permute-start | bytes 73736 | tf_op jit(solution)/shard_map/while/body/eval_jaxpr/ppermute | solution.py:12
  539.8 13.6 %collective-permute-start.4 = (f32[16]{0:T(128)S(1)}, f32[16]{0:T(128)S(1)}, u32[]{:S(2)}, u32[]{:S(2)}) collective-permute-start(f32[16]{0:T(128)S(1)} %copy.45), channel_id=1, source_target_pairs={{480,0},{0,32},{32,64},{64,96},{96,128},{128,160},{160,192},{192,2... | collective-permute-start | bytes 200 | tf_op jit(solution)/shard_map/while/body/eval_jaxpr/ppermute | solution.py:12
  544.5 15.5 %collective-permute-start.8 = (f32[16,768]{1,0:T(8,128)S(1)}, f32[16,768]{1,0:T(8,128)S(1)}, u32[]{:S(2)}, u32[]{:S(2)}) collective-permute-start(f32[16,768]{1,0:T(8,128)S(1)} %convolution_add_fusion.3), channel_id=1, source_target_pairs={{480,0},{0,32},{32,64},{64,96},{96,128},{128,160},{160,192},{192,2... | collective-permute-start | bytes 147464 | tf_op jit(solution)/shard_map/while/body/eval_jaxpr/ppermute | solution.py:12
  560.0 18.7 %collective-permute-start.6 = (f32[16]{0:T(128)S(1)}, f32[16]{0:T(128)S(1)}, u32[]{:S(2)}, u32[]{:S(2)}) collective-permute-start(f32[16]{0:T(128)S(1)} %copy.47), channel_id=1, source_target_pairs={{480,0},{0,32},{32,64},{64,96},{96,128},{128,160},{160,192},{192,2... | collective-permute-start | bytes 200 | tf_op jit(solution)/shard_map/while/body/eval_jaxpr/ppermute | solution.py:12
  561.9 23.3 %collective-permute-start.3 = (bf16[16,768]{1,0:T(8,128)(2,1)S(1)}, bf16[16,768]{1,0:T(8,128)(2,1)S(1)}, u32[]{:S(2)}, u32[]{:S(2)}) collective-permute-start(bf16[16,768]{1,0:T(8,128)(2,1)S(1)} %copy.44), channel_id=1, source_target_pairs={{480,0},{0,32},{32,64},{64,96},{96,128},{128,160},{160,192},{192,2... | collective-permute-start | bytes 73736 | tf_op jit(solution)/shard_map/while/body/eval_jaxpr/ppermute | solution.py:12
  569.8 15.5 %collective-permute-start.8 = (f32[16,768]{1,0:T(8,128)S(1)}, f32[16,768]{1,0:T(8,128)S(1)}, u32[]{:S(2)}, u32[]{:S(2)}) collective-permute-start(f32[16,768]{1,0:T(8,128)S(1)} %convolution_add_fusion.3), channel_id=1, source_target_pairs={{480,0},{0,32},{32,64},{64,96},{96,128},{128,160},{160,192},{192,2... | collective-permute-start | bytes 147464 | tf_op jit(solution)/shard_map/while/body/eval_jaxpr/ppermute | solution.py:12
  585.3 18.7 %collective-permute-start.6 = (f32[16]{0:T(128)S(1)}, f32[16]{0:T(128)S(1)}, u32[]{:S(2)}, u32[]{:S(2)}) collective-permute-start(f32[16]{0:T(128)S(1)} %copy.47), channel_id=1, source_target_pairs={{480,0},{0,32},{32,64},{64,96},{96,128},{128,160},{160,192},{192,2... | collective-permute-start | bytes 200 | tf_op jit(solution)/shard_map/while/body/eval_jaxpr/ppermute | solution.py:12
  587.2 23.3 %collective-permute-start.3 = (bf16[16,768]{1,0:T(8,128)(2,1)S(1)}, bf16[16,768]{1,0:T(8,128)(2,1)S(1)}, u32[]{:S(2)}, u32[]{:S(2)}) collective-permute-start(bf16[16,768]{1,0:T(8,128)(2,1)S(1)} %copy.44), channel_id=1, source_target_pairs={{480,0},{0,32},{32,64},{64,96},{96,128},{128,160},{160,192},{192,2... | collective-permute-start | bytes 73736 | tf_op jit(solution)/shard_map/while/body/eval_jaxpr/ppermute | solution.py:12
  590.3 13.6 %collective-permute-start.4 = (f32[16]{0:T(128)S(1)}, f32[16]{0:T(128)S(1)}, u32[]{:S(2)}, u32[]{:S(2)}) collective-permute-start(f32[16]{0:T(128)S(1)} %copy.45), channel_id=1, source_target_pairs={{480,0},{0,32},{32,64},{64,96},{96,128},{128,160},{160,192},{192,2... | collective-permute-start | bytes 200 | tf_op jit(solution)/shard_map/while/body/eval_jaxpr/ppermute | solution.py:12
  595.0 15.5 %collective-permute-start.8 = (f32[16,768]{1,0:T(8,128)S(1)}, f32[16,768]{1,0:T(8,128)S(1)}, u32[]{:S(2)}, u32[]{:S(2)}) collective-permute-start(f32[16,768]{1,0:T(8,128)S(1)} %convolution_add_fusion.3), channel_id=1, source_target_pairs={{480,0},{0,32},{32,64},{64,96},{96,128},{128,160},{160,192},{192,2... | collective-permute-start | bytes 147464 | tf_op jit(solution)/shard_map/while/body/eval_jaxpr/ppermute | solution.py:12
  610.5 18.7 %collective-permute-start.6 = (f32[16]{0:T(128)S(1)}, f32[16]{0:T(128)S(1)}, u32[]{:S(2)}, u32[]{:S(2)}) collective-permute-start(f32[16]{0:T(128)S(1)} %copy.47), channel_id=1, source_target_pairs={{480,0},{0,32},{32,64},{64,96},{96,128},{128,160},{160,192},{192,2... | collective-permute-start | bytes 200 | tf_op jit(solution)/shard_map/while/body/eval_jaxpr/ppermute | solution.py:12
  612.5 23.3 %collective-permute-start.3 = (bf16[16,768]{1,0:T(8,128)(2,1)S(1)}, bf16[16,768]{1,0:T(8,128)(2,1)S(1)}, u32[]{:S(2)}, u32[]{:S(2)}) collective-permute-start(bf16[16,768]{1,0:T(8,128)(2,1)S(1)} %copy.44), channel_id=1, source_target_pairs={{480,0},{0,32},{32,64},{64,96},{96,128},{128,160},{160,192},{192,2... | collective-permute-start | bytes 73736 | tf_op jit(solution)/shard_map/while/body/eval_jaxpr/ppermute | solution.py:12
  615.6 13.6 %collective-permute-start.4 = (f32[16]{0:T(128)S(1)}, f32[16]{0:T(128)S(1)}, u32[]{:S(2)}, u32[]{:S(2)}) collective-permute-start(f32[16]{0:T(128)S(1)} %copy.45), channel_id=1, source_target_pairs={{480,0},{0,32},{32,64},{64,96},{96,128},{128,160},{160,192},{192,2... | collective-permute-start | bytes 200 | tf_op jit(solution)/shard_map/while/body/eval_jaxpr/ppermute | solution.py:12
  620.3 15.5 %collective-permute-start.8 = (f32[16,768]{1,0:T(8,128)S(1)}, f32[16,768]{1,0:T(8,128)S(1)}, u32[]{:S(2)}, u32[]{:S(2)}) collective-permute-start(f32[16,768]{1,0:T(8,128)S(1)} %convolution_add_fusion.3), channel_id=1, source_target_pairs={{480,0},{0,32},{32,64},{64,96},{96,128},{128,160},{160,192},{192,2... | collective-permute-start | bytes 147464 | tf_op jit(solution)/shard_map/while/body/eval_jaxpr/ppermute | solution.py:12
  (87 other events, 710.2 us)
Sparse Core Ops, SparseCore 0:
  655.1 478.0 all-reduce.1
where the time goes:
time: 1150 us; the launch traced here: 1140 us
  waiting for transfers between devices  696 us (61%)
  starting transfers between devices  368 us (32%)
  local copies, waits for them, and re-layouts  30.9 us (3%)
  matrix products  27 us (2%)
  between operations  14.1 us (1%)
    psum x1, waiting for transfers between devices, per_device(): book_total = lax.psum(book_grad, ('db', 'pb'))  477 us
    ppermute x144, starting transfers between devices, shifted(): return lax.ppermute(block, axis, route)  368 us
    ppermute x144, waiting for transfers between devices, shifted(): return lax.ppermute(block, axis, route)  219 us
  transfers between devices with their start and end apart: 145, of which 65 were waited for; matrix products, arithmetic and copies ran while one was open for 2% of the time, Pallas kernels for 0%

commit v1 on v0

v1 whole, which is shorter than its diff:
```python
import functools
import math

import jax
import jax.numpy as jnp
from jax import lax
from jax.experimental import pallas as pl
from jax.experimental.pallas import tpu as pltpu
from jax.sharding import PartitionSpec as P

LANES = 128


def pack_kernel(queries_ref, codes_ref, weight_ref, positive_ref, out_ref):
    rows, width = queries_ref.shape
    books = codes_ref.shape[1]
    for j in range(width // LANES):
        out_ref[rows * j : rows * (j + 1), :] = queries_ref[:, LANES * j : LANES * (j + 1)]
    top = rows * (width // LANES)
    code_rows = codes_ref[...].astype(jnp.float32).T
    out_ref[top : top + books, :] = code_rows.astype(jnp.bfloat16)
    spot = lax.broadcasted_iota(jnp.int32, (rows, rows), 0)
    lane = lax.broadcasted_iota(jnp.int32, (rows, rows), 1)

    def column(row):
        spread = jnp.broadcast_to(row, (rows, rows))
        return jnp.sum(jnp.where(spot == lane, spread, 0.0), axis=1, keepdims=True)

    weight = column(weight_ref[...])
    positive = positive_ref[...]
    first = weight.astype(jnp.bfloat16).astype(jnp.float32)
    second = (weight - first).astype(jnp.bfloat16).astype(jnp.float32)
    third = weight - first - second
    block = column((positive // LANES).astype(jnp.float32))
    place = column((positive % LANES).astype(jnp.float32))
    wide = lax.broadcasted_iota(jnp.int32, (rows, LANES), 1)
    extra = jnp.zeros((rows, LANES), jnp.float32)
    for j, value in enumerate((first, second, third, block, place)):
        extra = jnp.where(wide == j, value, extra)
    out_ref[top + books :, :] = extra.astype(jnp.bfloat16)


def main_kernel(
    scale, me_ref, group_ref, cb_ref, codes_ref,
    loss_ref, gq_ref, gb_ref,
    code_scr, cb_scr, q_scr, dec_scr, s_scr, total_scr,
):
    members, _, _ = group_ref.shape
    width = cb_ref.shape[0]
    books = codes_ref.shape[1]
    rows = gq_ref.shape[0]
    blocks = width // LANES
    top = rows * blocks
    queries = members * rows
    me = me_ref[0, 0]
    code_scr[...] = group_ref[:, top : top + books, :].astype(jnp.float32).astype(jnp.int32)
    cb_scr[...] = cb_ref[...].astype(jnp.float32)
    for j in range(blocks):
        q_scr[:, LANES * j : LANES * (j + 1)] = group_ref[
            :, rows * j : rows * (j + 1), :
        ].reshape(queries, LANES)
    low_rows = lax.broadcasted_iota(jnp.int32, (8, LANES), 0) < 4

    def decode_block(d, carry):
        for four in range(books // 4):
            tiles = []
            for pair in (2 * four, 2 * four + 1):
                first = jnp.broadcast_to(code_scr[d, 2 * pair : 2 * pair + 1, :], (8, LANES))
                second = jnp.broadcast_to(
                    code_scr[d, 2 * pair + 1 : 2 * pair + 2, :], (8, LANES)
                )
                for t, index in enumerate((first, jnp.where(low_rows, first, second), second)):
                    at = 24 * pair + 8 * t
                    inner = index & (LANES - 1)
                    low = jnp.take_along_axis(cb_scr[at : at + 8, :LANES], inner, axis=1)
                    high = jnp.take_along_axis(cb_scr[at : at + 8, LANES:], inner, axis=1)
                    tiles.append(jnp.where(index >= LANES, high, low))
            dec_scr[d, 48 * four : 48 * four + 48, :] = jnp.concatenate(tiles, axis=0).astype(
                jnp.bfloat16
            )
        s_scr[d] = (
            jnp.dot(q_scr[...], dec_scr[d], preferred_element_type=jnp.float32) * scale
        )
        return carry

    lax.fori_loop(0, members, decode_block, 0)

    highest = s_scr[0]
    for d in range(1, members):
        highest = jnp.maximum(highest, s_scr[d])
    row_max = jnp.max(highest, axis=1, keepdims=True)
    total = jnp.exp(s_scr[0] - row_max)
    for d in range(1, members):
        total = total + jnp.exp(s_scr[d] - row_max)
    log_total = row_max + jnp.log(jnp.sum(total, axis=1, keepdims=True))
    total_scr[...] = jnp.broadcast_to(log_total, (queries, LANES))

    def extras(block):
        weight = block[:, 0:1] + block[:, 1:2] + block[:, 2:3]
        return weight, block[:, 3:4], block[:, 4:5]

    extra = group_ref[:, top + books :, :].reshape(queries, LANES).astype(jnp.float32)
    weight, block, place = extras(extra)
    here = me.astype(jnp.float32)
    lane = lax.broadcasted_iota(jnp.int32, (queries, LANES), 1).astype(jnp.float32)
    is_positive = jnp.where((block == here) & (place == lane), 1.0, 0.0)
    coefficient = (
        weight * (jnp.exp(s_scr[me] - total_scr[...]) - is_positive) * scale
    ).astype(jnp.bfloat16)
    passage_grad = lax.dot_general(
        q_scr[...], coefficient, (((0,), (0,)), ((), ())), preferred_element_type=jnp.float32
    )

    own = pl.ds(pl.multiple_of(me * rows, rows), rows)
    weight, block, place = extras(group_ref[me, top + books :, :].astype(jnp.float32))
    own_total = total_scr[own, :]
    own_lane = lax.broadcasted_iota(jnp.int32, (rows, LANES), 1).astype(jnp.float32)
    chosen = jnp.zeros((rows, LANES), jnp.float32)
    grad = jnp.zeros((rows, width), jnp.float32)
    for d in range(members):
        scores = s_scr[d, own, :]
        hit = (block == float(d)) & (place == own_lane)
        chosen = chosen + jnp.where(hit, scores, 0.0)
        part = (
            weight * (jnp.exp(scores - own_total) - jnp.where(hit, 1.0, 0.0)) * scale
        ).astype(jnp.bfloat16)
        grad = grad + lax.dot_general(
            part, dec_scr[d], (((1,), (1,)), ((), ())), preferred_element_type=jnp.float32
        )
    gq_ref[...] = grad
    loss = weight * (own_total - jnp.sum(chosen, axis=1, keepdims=True))
    diagonal = lax.broadcasted_iota(jnp.int32, (rows, LANES), 0).astype(jnp.float32) == own_lane
    loss_ref[...] = jnp.sum(jnp.where(diagonal, loss, 0.0), axis=0, keepdims=True)[:, :rows]

    levels = cb_ref.shape[1]
    level = lax.broadcasted_iota(jnp.int32, (LANES, levels), 1)
    upper = lax.broadcasted_iota(jnp.int32, (24, LANES), 0) < 12
    for pair in range(books // 2):
        tables = [
            jnp.where(codes_ref[:, m : m + 1] == level, 1.0, 0.0).astype(jnp.bfloat16)
            for m in (2 * pair, 2 * pair + 1)
        ]
        terms = passage_grad[24 * pair : 24 * pair + 24, :]
        high = terms.astype(jnp.bfloat16).astype(jnp.float32)
        low = terms - high
        spread = [
            jnp.concatenate([jnp.where(upper, x, 0.0), jnp.where(upper, 0.0, x)], axis=1)
            for x in (high, low)
        ]
        sums = jnp.dot(
            jnp.concatenate(spread, axis=0).astype(jnp.bfloat16),
            jnp.concatenate(tables, axis=0),
            preferred_element_type=jnp.float32,
        )
        gb_ref[24 * pair : 24 * pair + 24, :] = sums[:24] + sums[24:]


def per_device(queries, passage_codes, codebooks, positives, loss_weight):
    rows, width = queries.shape
    passages, books = passage_codes.shape
    sub_width, levels = codebooks.shape[1:]
    members = lax.axis_size("db")
    others = lax.axis_size("pb")
    pack_rows = rows * (width // LANES) + books + rows
    scale = 2.5 / math.sqrt(width)
    pack = pl.pallas_call(
        pack_kernel,
        out_shape=jax.ShapeDtypeStruct((pack_rows, LANES), jnp.bfloat16),
        name="pack",
    )(queries, passage_codes, loss_weight.reshape(1, rows), positives.reshape(1, rows))
    group = lax.all_gather(pack, "db", axis=0)
    me = lax.axis_index("db").astype(jnp.int32).reshape(1, 1)
    loss, grad_queries, book_part = pl.pallas_call(
        functools.partial(main_kernel, scale),
        out_shape=(
            jax.ShapeDtypeStruct((1, rows), jnp.float32),
            jax.ShapeDtypeStruct((rows, width), jnp.float32),
            jax.ShapeDtypeStruct((width, levels), jnp.float32),
        ),
        in_specs=[pl.BlockSpec(memory_space=pltpu.SMEM)]
        + [pl.BlockSpec(memory_space=pltpu.VMEM)] * 3,
        scratch_shapes=[
            pltpu.VMEM((members, books, LANES), jnp.int32),
            pltpu.VMEM((width, levels), jnp.float32),
            pltpu.VMEM((members * rows, width), jnp.bfloat16),
            pltpu.VMEM((members, width, LANES), jnp.bfloat16),
            pltpu.VMEM((members, members * rows, LANES), jnp.float32),
            pltpu.VMEM((members * rows, LANES), jnp.float32),
        ],
        name="core",
    )(me, group, codebooks.reshape(width, levels), passage_codes)
    part = lax.all_to_all(book_part.reshape(members, -1, levels), "db", 0, 0)
    part = jnp.sum(part, axis=0)
    part = lax.all_to_all(part.reshape(others, -1), "pb", 0, 0)
    part = jnp.sum(part, axis=0)
    part = lax.all_gather(part, "pb", axis=0)
    part = lax.all_gather(part.reshape(-1, levels), "db", axis=0)
    return loss.reshape(rows), grad_queries, part.reshape(books, sub_width, levels)


def solution(mesh):
    return jax.shard_map(
        per_device,
        mesh=mesh,
        in_specs=(
            P(("db", "pb"), None),
            P(("db", "pb"), None),
            P(),
            P(("db", "pb")),
            P(("db", "pb")),
        ),
        out_specs=(P(("db", "pb")), P(("db", "pb"), None), P()),
        check_vma=False,
    )
```

time: 1150 us -> 181 us (0.16)
  waiting for transfers between devices: 696 us -> 0 us
  starting transfers between devices: 368 us -> 0 us
  blocking collectives: 0 us -> 159 us
  matrix products: 27 us -> 0 us
  local copies, waits for them, and re-layouts: 30.9 us -> 5.01 us
  Pallas kernels: 0 us -> 16 us
  between operations: 14.1 us -> 0.67 us
    psum x1 -> x0, waiting for transfers between devices: 477 us -> none  [per_device(): book_total = lax.psum(book_grad, ('db', 'pb'))]
    ppermute x144 -> x0, starting transfers between devices: 368 us -> none  [shifted(): return lax.ppermute(block, axis, route)]
    ppermute x144 -> x0, waiting for transfers between devices: 219 us -> none  [shifted(): return lax.ppermute(block, axis, route)]
    all_gather x0 -> x3, blocking collectives: none -> 113 us  [the longest x1 45 us: per_device(): part = lax.all_gather(part, 'pb', axis=0)]
    all_to_all x0 -> x2, blocking collectives: none -> 45.7 us  [the longest x1 27.8 us: per_device(): part = lax.all_to_all(part.reshape(others, -1), 'pb', 0, 0)]
    dot_general x112 -> x0, matrix products: 27 us -> none  [the longest x16 5.67 us: grad_step(): jnp.einsum('qd,qp->dp', query_block, coefficient, preferred_element_type=...]
    eq x32 -> x0, local copies, waits for them, and re-layouts: 22 us -> none  [code_table(): return (levels[None, :, None] == code_rows[:, None, :]).astype(jnp.bfloat16)]
    pallas_call x0 -> x2, Pallas kernels: none -> 16 us  [the longest x1 14.4 us: per_device(): pl.pallas_call(functools.partial(main_kernel, scale), out_shape=(jax.Shap...]
  transfers between devices with their start and end apart: 145 -> 0, of which waited for: 65 -> 0; matrix products, arithmetic and copies ran while one was open for 2% -> 0% of each run, Pallas kernels for 0% -> 0%
where the time goes in v1:
time: 181 us
  blocking collectives  159 us (88%)
  Pallas kernels  16 us (9%)
  local copies, waits for them, and re-layouts  5.01 us (3%)
    all_gather x1, blocking collectives, per_device(): part = lax.all_gather(part, 'pb', axis=0)  45 us
    all_gather x1, blocking collectives, per_device(): part = lax.all_gather(part.reshape(-1, levels), 'db', axis=0)  38.8 us
    all_gather x1, blocking collectives, per_device(): group = lax.all_gather(pack, 'db', axis=0)  29.5 us
    all_to_all x1, blocking collectives, per_device(): part = lax.all_to_all(part.reshape(others, -1), 'pb', 0, 0)  27.8 us
    all_to_all x1, blocking collectives, per_device(): part = lax.all_to_all(book_part.reshape(members, -1, levels), 'db', 0, 0)  17.9 us
    pallas_call x1, Pallas kernels, per_device(): pl.pallas_call(functools.partial(main_kernel, scale), out_shape=(jax.Shap...  14.4 us
    unnamed x4, local copies, waits for them, and re-layouts  4.04 us

profile of v1, /device:TPU:1, one launch (start us, length us, event | category | flops | bytes accessed | tf_op | source)
XLA Modules:
  0.0 181.0 jit_solution(17452055449882010016)
XLA Ops:
  0.6 1.5 copy.15.codes_ref
  2.1 1.2 copy.16
  3.3 0.8 reshape.34.cb_ref
  4.2 1.6 pack.1
  5.7 29.5 %all-gather = bf16[2816,128]{1,0:T(8,128)(2,1)} all-gather(bf16[176,128]{1,0:T(8,128)(2,1)} %pack.1), channel_id=2, replica_groups=mesh['db'=16,'pb'=32] {'db'}, dimensions={0}, use_global_device_ids=true | all-gather | bytes 765952 | tf_op jit(solution)/shard_map/all_gather | solution.py:171
  35.2 14.4 %core.1 = (f32[1,16]{1,0:T(1,128)}, f32[16,768]{1,0:T(8,128)}, f32[768,256]{1,0:T(8,128)}) custom-call(s32[1,1]{1,0:T(1,128)} %bitcast.me_ref, bf16[16,176,128]{2,1,0:T(8,128)(2,1)} %bitcast.6, bf16[768,256]{1,0:T(8,128)(2,1)} %reshape.34.cb_ref, s32[128,64]{1,0:T(8,128)} %copy.15.codes_ref), custom_call_target="tpu_custom_call" | custom-call | tf_op jit(solution)/shard_map/core/pallas_call | solution.py:173
  49.7 17.9 %all_to_all.14 = f32[16,48,256]{2,1,0:T(8,128)S(1)} all-to-all(f32[16,48,256]{2,1,0:T(8,128)} %bitcast.7), channel_id=1, replica_groups=mesh['db'=16,'pb'=32] {'db'}, dimensions={0} | all-to-all | bytes 1572864 | tf_op jit(solution)/shard_map/all_to_all | solution.py:192
  67.6 0.1 reduce_sum.18
  67.7 0.1 all_to_all.10
  67.7 27.8 %all_to_all.15 = f32[32,1,384]{2,1,0:T(1,128)S(1)} all-to-all(f32[32,1,384]{2,1,0:T(1,128)S(1)} %all_to_all.10), channel_id=1, replica_groups=mesh['db'=16,'pb'=32] {'pb'}, dimensions={0} | all-to-all | bytes 98304 | tf_op jit(solution)/shard_map/all_to_all | solution.py:194
  95.5 0.1 reduce_sum.19
  95.6 45.0 %all-gather.2 = f32[32,1,384]{2,1,0:T(1,128)S(1)} all-gather(f32[1,1,384]{2,1,0:T(1,128)S(1)} %reshape.41), channel_id=3, replica_groups=mesh['db'=16,'pb'=32] {'pb'}, dimensions={0}, use_global_device_ids=true | all-gather | bytes 50688 | tf_op jit(solution)/shard_map/all_gather | solution.py:196
  140.6 0.1 reduce.1
  140.8 38.8 %all_gather.19 = f32[16,48,256]{2,1,0:T(8,128)S(1)} all-gather(f32[1,48,256]{2,1,0:T(8,128)S(1)} %all_gather_reshape.3), channel_id=1, replica_groups=mesh['db'=16,'pb'=32] {'db'}, dimensions={0}, use_global_device_ids=true | all-gather | bytes 835584 | tf_op jit(solution)/shard_map/all_gather | solution.py:197
  179.6 0.1 reshape.37
  179.7 1.3 copy.18
  (2 shorter events, 0.0 us)

commit v2 on v1

--- a/solution.py
+++ b/solution.py
@@ -135,6 +135,7 @@
     levels = cb_ref.shape[1]
     level = lax.broadcasted_iota(jnp.int32, (LANES, levels), 1)
     upper = lax.broadcasted_iota(jnp.int32, (24, LANES), 0) < 12
+    ready = []
     for pair in range(books // 2):
         tables = [
             jnp.where(codes_ref[:, m : m + 1] == level, 1.0, 0.0).astype(jnp.bfloat16)
@@ -152,7 +153,17 @@
             jnp.concatenate(tables, axis=0),
             preferred_element_type=jnp.float32,
         )
-        gb_ref[24 * pair : 24 * pair + 24, :] = sums[:24] + sums[24:]
+        ready.append(sums[:24] + sums[24:])
+        if pair % 2 == 1:
+            gb_ref[24 * pair - 24 : 24 * pair + 24, :] = jnp.concatenate(ready, axis=0).astype(
+                jnp.bfloat16
+            )
+            ready = []
+
+
+def spread(block, axis):
+    copies = jnp.broadcast_to(block[None], (lax.axis_size(axis),) + block.shape)
+    return lax.all_to_all(copies, axis, 0, 0)
 
 
 def per_device(queries, passage_codes, codebooks, positives, loss_weight):
@@ -168,14 +179,14 @@
         out_shape=jax.ShapeDtypeStruct((pack_rows, LANES), jnp.bfloat16),
         name="pack",
     )(queries, passage_codes, loss_weight.reshape(1, rows), positives.reshape(1, rows))
-    group = lax.all_gather(pack, "db", axis=0)
+    group = spread(pack, "db")
     me = lax.axis_index("db").astype(jnp.int32).reshape(1, 1)
     loss, grad_queries, book_part = pl.pallas_call(
         functools.partial(main_kernel, scale),
         out_shape=(
             jax.ShapeDtypeStruct((1, rows), jnp.float32),
             jax.ShapeDtypeStruct((rows, width), jnp.float32),
-            jax.ShapeDtypeStruct((width, levels), jnp.float32),
+            jax.ShapeDtypeStruct((width, levels), jnp.bfloat16),
         ),
         in_specs=[pl.BlockSpec(memory_space=pltpu.SMEM)]
         + [pl.BlockSpec(memory_space=pltpu.VMEM)] * 3,
@@ -190,11 +201,11 @@
         name="core",
     )(me, group, codebooks.reshape(width, levels), passage_codes)
     part = lax.all_to_all(book_part.reshape(members, -1, levels), "db", 0, 0)
-    part = jnp.sum(part, axis=0)
+    part = jnp.sum(part.astype(jnp.float32), axis=0)
     part = lax.all_to_all(part.reshape(others, -1), "pb", 0, 0)
     part = jnp.sum(part, axis=0)
-    part = lax.all_gather(part, "pb", axis=0)
-    part = lax.all_gather(part.reshape(-1, levels), "db", axis=0)
+    part = spread(part, "pb").reshape(-1, levels).astype(jnp.bfloat16)
+    part = spread(part, "db").astype(jnp.float32)
     return loss.reshape(rows), grad_queries, part.reshape(books, sub_width, levels)
 
 

time: 181 us -> 121 us (0.67)
  blocking collectives: 159 us -> 72.1 us
  waiting for transfers between devices: 0 us -> 12.5 us
  starting transfers between devices: 0 us -> 10.4 us
  local copies, waits for them, and re-layouts: 5.01 us -> 7.52 us
    all_gather x3 -> x0, blocking collectives: 113 us -> none  [the longest x1 45 us: per_device(): part = lax.all_gather(part, 'pb', axis=0)]
    all_to_all x0 -> x2, blocking collectives: none -> 31.8 us  [spread(): return lax.all_to_all(copies, axis, 0, 0)]
    all_to_all x0 -> x1, waiting for transfers between devices: none -> 12.5 us  [spread(): return lax.all_to_all(copies, axis, 0, 0)]
    all_to_all x0 -> x1, starting transfers between devices: none -> 10.4 us  [spread(): return lax.all_to_all(copies, axis, 0, 0)]
    all_to_all x1, blocking collectives: 17.9 us -> 14.1 us  [per_device(): part = lax.all_to_all(book_part.reshape(members, -1, levels), 'db', 0, 0)]
    broadcast_in_dim x0 -> x4, local copies, waits for them, and re-layouts: none -> 2.31 us  [spread(): copies = jnp.broadcast_to(block[None], (lax.axis_size(axis),) + block.shape)]
    unnamed x4 -> x9, local copies, waits for them, and re-layouts: 4.04 us -> 4.09 us
  transfers between devices with their start and end apart: 0 -> 1, of which waited for: 0 -> 1; matrix products, arithmetic and copies ran while one was open for 0% -> 1% of each run, Pallas kernels for 0% -> 0%
where the time goes in v2:
time: 121 us; the launch traced here: 120 us
  blocking collectives  72.1 us (60%)
  Pallas kernels  15.9 us (13%)
  waiting for transfers between devices  12.5 us (10%)
  starting transfers between devices  10.4 us (9%)
  local copies, waits for them, and re-layouts  7.52 us (6%)
    all_to_all x2, blocking collectives, spread(): return lax.all_to_all(copies, axis, 0, 0)  31.8 us
    all_to_all x1, blocking collectives, per_device(): part = lax.all_to_all(part.reshape(others, -1), 'pb', 0, 0)  26.1 us
    pallas_call x1, Pallas kernels, per_device(): pl.pallas_call(functools.partial(main_kernel, scale), out_shape=(jax.Shap...  14.3 us
    all_to_all x1, blocking collectives, per_device(): part = lax.all_to_all(book_part.reshape(members, -1, levels), 'db', 0, 0)  14.1 us
    all_to_all x1, waiting for transfers between devices, spread(): return lax.all_to_all(copies, axis, 0, 0)  12.5 us
    all_to_all x1, starting transfers between devices, spread(): return lax.all_to_all(copies, axis, 0, 0)  10.4 us
    unnamed x9, local copies, waits for them, and re-layouts  4.09 us
  transfers between devices with their start and end apart: 1, of which 1 were waited for; matrix products, arithmetic and copies ran while one was open for 1% of the time, Pallas kernels for 0%

profile of v2, /device:TPU:1, one launch (start us, length us, event | category | flops | bytes accessed | tf_op | source)
XLA Modules:
  0.0 120.0 jit_solution(4835682931604615102)
XLA Ops:
  0.6 1.5 %copy.15.codes_ref = s32[128,64]{1,0:T(8,128)} copy(s32[128,64]{0,1:T(8,128)} %param.6) | data formatting | bytes 65536 | tf_op args[1]
  2.1 1.6 %pack.1 = bf16[176,128]{1,0:T(8,128)(2,1)} custom-call(bf16[16,768]{1,0:T(8,128)(2,1)} %queries_ref.1, s32[128,64]{1,0:T(8,128)} %copy.15.codes_ref, f32[1,16]{1,0:T(1,128)} %bitcast.6, s32[1,16]{1,0:T(1,128)} %bitcast.7), custom_call_target="tpu_custom_call" | custom-call | tf_op jit(solution)/shard_map/pack/pallas_call | solution.py:177
  3.7 1.7 %broadcast_in_dim.6 = bf16[16,176,128]{2,1,0:T(8,128)(2,1)} broadcast(bf16[176,128]{1,0:T(8,128)(2,1)} %pack.1), dimensions={1,2} | broadcast | bytes 765952 | tf_op jit(solution)/shard_map/broadcast_in_dim | solution.py:165
  5.4 0.0 copy-start.1
  5.4 10.4 %all-to-all-start = ((bf16[16,176,128]{2,1,0:T(8,128)(2,1)}), bf16[16,176,128]{2,1,0:T(8,128)(2,1)S(1)}, u32[]{:S(2)}, u32[]{:S(2)}) async-start(bf16[16,176,128]{2,1,0:T(8,128)(2,1)} %broadcast_in_dim.6), calls=%async_computation | async-start | bytes 1441792 | tf_op jit(solution)/shard_map/all_to_all | solution.py:166
  15.8 0.0 copy-done.1
  15.8 0.2 copy.16
  16.0 0.8 reshape.52.cb_ref
  16.8 12.5 %all-to-all-done.group_ref = bf16[16,176,128]{2,1,0:T(8,128)(2,1)S(1)} async-done(((bf16[16,176,128]{2,1,0:T(8,128)(2,1)}), bf16[16,176,128]{2,1,0:T(8,128)(2,1)S(1)}, u32[]{:S(2)}, u32[]{:S(2)}) %all-to-all-start) | async-done | bytes 720928 | tf_op jit(solution)/shard_map/all_to_all | solution.py:166
  29.4 0.0 copy-start
  29.4 0.9 copy-done
  30.2 14.3 %core.1 = (f32[1,16]{1,0:T(1,128)}, f32[16,768]{1,0:T(8,128)}, bf16[768,256]{1,0:T(8,128)(2,1)}) custom-call(s32[1,1]{1,0:T(1,128)} %bitcast.me_ref, bf16[16,176,128]{2,1,0:T(8,128)(2,1)} %copy-done, bf16[768,256]{1,0:T(8,128)(2,1)} %reshape.52.cb_ref, s32[128,64]{1,0:T(8,128)} %copy.15.codes_ref), custom_call_target="tpu_custom_call" | custom-call | tf_op jit(solution)/shard_map/core/pallas_call | solution.py:184
  44.6 14.1 %all_to_all.30 = bf16[16,48,256]{2,1,0:T(8,128)(2,1)S(1)} all-to-all(bf16[16,48,256]{2,1,0:T(8,128)(2,1)} %bitcast.5), channel_id=1, replica_groups=mesh['db'=16,'pb'=32] {'db'}, dimensions={0} | all-to-all | bytes 786432 | tf_op jit(solution)/shard_map/all_to_all | solution.py:203
  58.7 0.1 convert_reduce_fusion
  58.8 0.1 all_to_all.21
  58.8 26.1 %all_to_all.31 = f32[32,1,384]{2,1,0:T(1,128)S(1)} all-to-all(f32[32,1,384]{2,1,0:T(1,128)S(1)} %all_to_all.21), channel_id=1, replica_groups=mesh['db'=16,'pb'=32] {'pb'}, dimensions={0} | all-to-all | bytes 98304 | tf_op jit(solution)/shard_map/all_to_all | solution.py:205
  84.9 0.1 reduce_sum.19
  85.0 0.5 broadcast.5
  85.6 0.8 reduce.3
  86.3 0.1 reshape.60
  86.4 15.5 %all_to_all.32 = bf16[32,2,192]{2,1,0:T(2,128)(2,1)S(1)} all-to-all(bf16[32,2,192]{2,1,0:T(2,128)(2,1)S(1)} %reshape.60), channel_id=1, replica_groups=mesh['db'=16,'pb'=32] {'pb'}, dimensions={0} | all-to-all | bytes 49152 | tf_op jit(solution)/shard_map/all_to_all | solution.py:166
  101.9 0.1 reshape.61
  102.0 0.1 convert_reduce_fusion.1
  102.2 16.3 %all_to_all.33 = bf16[16,48,256]{2,1,0:T(8,128)(2,1)S(1)} all-to-all(bf16[16,48,256]{2,1,0:T(8,128)(2,1)S(1)} %broadcast_in_dim.8), channel_id=1, replica_groups=mesh['db'=16,'pb'=32] {'db'}, dimensions={0} | all-to-all | bytes 786432 | tf_op jit(solution)/shard_map/all_to_all | solution.py:166
  118.6 0.1 reshape.58
  118.6 1.3 %copy.18 = f32[64,12,256]{2,0,1:T(8,128)} copy(f32[64,12,256]{2,1,0:T(8,128)S(1)} %reshape.58) | data formatting | bytes 1572864
  (3 shorter events, 0.1 us)
Async XLA Ops:
  5.4 10.4 %copy-start.1 = (bf16[64,12,256]{2,0,1:T(8,128)(2,1)S(1)}, bf16[64,12,256]{2,0,1:T(8,128)(2,1)}, u32[]{:S(2)}) copy-start(bf16[64,12,256]{2,0,1:T(8,128)(2,1)} %param.7) | copy-start | bytes 1179652
  5.4 24.0 %all-to-all-start = ((bf16[16,176,128]{2,1,0:T(8,128)(2,1)}), bf16[16,176,128]{2,1,0:T(8,128)(2,1)S(1)}, u32[]{:S(2)}, u32[]{:S(2)}) async-start(bf16[16,176,128]{2,1,0:T(8,128)(2,1)} %broadcast_in_dim.6), calls=%async_computation | async-start | bytes 1441792 | tf_op jit(solution)/shard_map/all_to_all | solution.py:166
  29.4 0.9 copy-start

commit v3 on v1

v3 whole, which is shorter than its diff:
```python
import functools
import math

import jax
import jax.numpy as jnp
from jax import lax
from jax.experimental import pallas as pl
from jax.experimental.pallas import tpu as pltpu
from jax.sharding import Mesh
from jax.sharding import PartitionSpec as P

LANES = 128
PLANE = ("db", "near")
WHOLE = ("db", "near", "ring")


def order_table(width, books, inverse):
    sub_width = width // books
    row = lax.broadcasted_iota(jnp.int32, (width, width), 0)
    column = lax.broadcasted_iota(jnp.int32, (1, width), 1)
    if inverse:
        source = (column % sub_width) * books + column // sub_width
    else:
        source = (column % books) * sub_width + column // books
    return jnp.where(row == source, 1.0, 0.0).astype(jnp.bfloat16)


def pack_kernel(queries_ref, codes_ref, weight_ref, positive_ref, out_ref):
    rows, width = queries_ref.shape
    books = codes_ref.shape[0]
    top = rows * (width // LANES)
    sorted_rows = jnp.dot(
        queries_ref[...], order_table(width, books, False), preferred_element_type=jnp.float32
    ).astype(jnp.bfloat16)
    code_rows = codes_ref[...].astype(jnp.float32).astype(jnp.bfloat16)
    spot = lax.broadcasted_iota(jnp.int32, (rows, rows), 0)
    lane = lax.broadcasted_iota(jnp.int32, (rows, rows), 1)

    def column(row):
        spread_row = jnp.broadcast_to(row, (rows, rows))
        return jnp.sum(jnp.where(spot == lane, spread_row, 0.0), axis=1, keepdims=True)

    weight = column(weight_ref[...])
    positive = positive_ref[...]
    first = weight.astype(jnp.bfloat16).astype(jnp.float32)
    second = (weight - first).astype(jnp.bfloat16).astype(jnp.float32)
    third = weight - first - second
    block = column((positive // LANES).astype(jnp.float32))
    place = column((positive % LANES).astype(jnp.float32))
    wide = lax.broadcasted_iota(jnp.int32, (rows, LANES), 1)
    extra = jnp.zeros((rows, LANES), jnp.float32)
    for j, value in enumerate((first, second, third, block, place)):
        extra = jnp.where(wide == j, value, extra)
    extra = extra.astype(jnp.bfloat16)
    for d in range(out_ref.shape[0]):
        for j in range(width // LANES):
            out_ref[d, rows * j : rows * (j + 1), :] = sorted_rows[:, LANES * j : LANES * (j + 1)]
        out_ref[d, top : top + books, :] = code_rows
        out_ref[d, top + books :, :] = extra


def main_kernel(
    scale, books, me_ref, group_ref, cb_ref,
    loss_ref, gq_ref, gb_ref,
    cb_scr, q_scr, dec_scr, s_scr, max_scr, sum_scr, total_scr, pg_scr, gb_scr,
):
    members = group_ref.shape[0]
    width, levels = cb_ref.shape
    sub_width = width // books
    rows = gq_ref.shape[0]
    blocks = width // LANES
    top = rows * blocks
    queries = members * rows
    me = me_ref[0, 0]
    cb_scr[...] = cb_ref[...].astype(jnp.float32)
    for j in range(blocks):
        q_scr[:, LANES * j : LANES * (j + 1)] = group_ref[
            :, rows * j : rows * (j + 1), :
        ].reshape(queries, LANES)

    def decode(t):
        for side in range(2):
            codes = (
                group_ref[2 * t + side, top : top + books, :]
                .astype(jnp.float32)
                .astype(jnp.int32)
            )
            for two in range(books // 16):
                index = [codes[16 * two + 8 * h : 16 * two + 8 * h + 8, :] for h in range(2)]
                inner = [x & (LANES - 1) for x in index]
                upper = [x >= LANES for x in index]
                for c in range(sub_width):
                    tiles = []
                    for h in range(2):
                        at = c * books + 16 * two + 8 * h
                        low = jnp.take_along_axis(cb_scr[at : at + 8, :LANES], inner[h], axis=1)
                        high = jnp.take_along_axis(cb_scr[at : at + 8, LANES:], inner[h], axis=1)
                        tiles.append(jnp.where(upper[h], high, low))
                    at = c * books + 16 * two
                    dec_scr[t, at : at + 16, LANES * side : LANES * side + LANES] = (
                        jnp.concatenate(tiles, axis=0).astype(jnp.bfloat16)
                    )

    def score(t):
        both = jnp.dot(q_scr[...], dec_scr[t], preferred_element_type=jnp.float32) * scale
        left, right = both[:, :LANES], both[:, LANES:]
        s_scr[2 * t] = left
        s_scr[2 * t + 1] = right
        newest = jnp.maximum(left, right)
        if t > 0:
            before = max_scr[...]
            newest = jnp.maximum(newest, before)
        total = jnp.exp(left - newest) + jnp.exp(right - newest)
        if t > 0:
            total = total + sum_scr[...] * jnp.exp(before - newest)
        max_scr[...] = newest
        sum_scr[...] = total

    for t in range(members // 2):
        decode(t)
        score(t)

    highest = max_scr[...]
    row_max = jnp.max(highest, axis=1, keepdims=True)
    total = jnp.sum(sum_scr[...] * jnp.exp(highest - row_max), axis=1, keepdims=True)
    total_scr[...] = jnp.broadcast_to(row_max + jnp.log(total), (queries, LANES))

    def extras(block):
        weight = block[:, 0:1] + block[:, 1:2] + block[:, 2:3]
        return weight, block[:, 3:4], block[:, 4:5]

    extra = group_ref[:, top + books :, :].reshape(queries, LANES).astype(jnp.float32)
    weight, block, place = extras(extra)
    here = me.astype(jnp.float32)
    lane = lax.broadcasted_iota(jnp.int32, (queries, LANES), 1).astype(jnp.float32)
    is_positive = jnp.where((block == here) & (place == lane), 1.0, 0.0)
    coefficient = (
        weight * (jnp.exp(s_scr[me] - total_scr[...]) - is_positive) * scale
    ).astype(jnp.bfloat16)
    pg_scr[:width, :] = lax.dot_general(
        q_scr[...], coefficient, (((0,), (0,)), ((), ())), preferred_element_type=jnp.float32
    )
    pg_scr[width:, :] = jnp.zeros((pg_scr.shape[0] - width, LANES), jnp.float32)

    own_codes = group_ref[me, top : top + books, :].astype(jnp.float32).astype(jnp.int32)
    level = lax.broadcasted_iota(jnp.int32, (levels, LANES), 0)
    nothing = jnp.zeros((16, LANES), jnp.float32)
    for m in range(0, books, 2):
        tables = [
            jnp.where(
                jnp.broadcast_to(own_codes[m + h : m + h + 1, :], (levels, LANES)) == level,
                1.0,
                0.0,
            ).astype(jnp.bfloat16)
            for h in range(2)
        ]
        parts = []
        for h in range(2):
            terms = pg_scr[pl.ds(m + h, 16, stride=books), :]
            high = terms.astype(jnp.bfloat16).astype(jnp.float32)
            for x in (high, terms - high):
                parts.append(
                    jnp.concatenate([x, nothing] if h == 0 else [nothing, x], axis=1)
                )
        sums = lax.dot_general(
            jnp.concatenate(parts, axis=0).astype(jnp.bfloat16),
            jnp.concatenate(tables, axis=1),
            (((1,), (1,)), ((), ())),
            preferred_element_type=jnp.float32,
        )
        for h in range(2):
            both = sums[32 * h : 32 * h + 16] + sums[32 * h + 16 : 32 * h + 32]
            for j in range(levels // LANES):
                gb_scr[j, pl.ds(m + h, 16, stride=books), :] = both[:, LANES * j : LANES * j + LANES]
    for j in range(levels // LANES):
        gb_ref[:, LANES * j : LANES * j + LANES] = gb_scr[j, :width, :].astype(jnp.bfloat16)

    own = pl.ds(pl.multiple_of(me * rows, rows), rows)
    weight, block, place = extras(group_ref[me, top + books :, :].astype(jnp.float32))
    own_total = total_scr[own, :]
    own_lane = lax.broadcasted_iota(jnp.int32, (rows, LANES), 1).astype(jnp.float32)
    chosen = jnp.zeros((rows, LANES), jnp.float32)
    grad = jnp.zeros((rows, width), jnp.float32)
    for t in range(members // 2):
        parts = []
        for d in (2 * t, 2 * t + 1):
            scores = s_scr[d, own, :]
            hit = (block == float(d)) & (place == own_lane)
            chosen = chosen + jnp.where(hit, scores, 0.0)
            parts.append(
                weight * (jnp.exp(scores - own_total) - jnp.where(hit, 1.0, 0.0)) * scale
            )
        grad = grad + lax.dot_general(
            jnp.concatenate(parts, axis=1).astype(jnp.bfloat16),
            dec_scr[t],
            (((1,), (1,)), ((), ())),
            preferred_element_type=jnp.float32,
        )
    first = grad.astype(jnp.bfloat16).astype(jnp.float32)
    second = (grad - first).astype(jnp.bfloat16).astype(jnp.float32)
    third = grad - first - second
    restored = jnp.dot(
        jnp.concatenate([first, second, third], axis=0).astype(jnp.bfloat16),
        order_table(width, books, True),
        preferred_element_type=jnp.float32,
    )
    gq_ref[...] = restored[:rows] + restored[rows : 2 * rows] + restored[2 * rows :]
    loss = weight * (own_total - jnp.sum(chosen, axis=1, keepdims=True))
    diagonal = lax.broadcasted_iota(jnp.int32, (rows, LANES), 0).astype(jnp.float32) == own_lane
    loss_ref[...] = jnp.sum(jnp.where(diagonal, loss, 0.0), axis=0, keepdims=True)[:, :rows]


def spread(block, axis):
    copies = jnp.broadcast_to(block[None], (lax.axis_size(axis),) + block.shape)
    return lax.all_to_all(copies, axis, 0, 0)


def per_device(queries, passage_codes, codebooks, positives, loss_weight):
    rows, width = queries.shape
    books = passage_codes.shape[1]
    sub_width, levels = codebooks.shape[1:]
    members = lax.axis_size("db")
    plane = lax.axis_size(PLANE)
    pack_rows = rows * (width // LANES) + books + rows
    scale = 2.5 / math.sqrt(width)
    pack = pl.pallas_call(
        pack_kernel,
        out_shape=jax.ShapeDtypeStruct((members, pack_rows, LANES), jnp.bfloat16),
        name="pack",
    )(queries, passage_codes.T, loss_weight.reshape(1, rows), positives.reshape(1, rows))
    group = lax.all_to_all(pack, "db", 0, 0)
    me = lax.axis_index("db").astype(jnp.int32).reshape(1, 1)
    loss, grad_queries, book_part = pl.pallas_call(
        functools.partial(main_kernel, scale, books),
        out_shape=(
            jax.ShapeDtypeStruct((1, rows), jnp.float32),
            jax.ShapeDtypeStruct((rows, width), jnp.float32),
            jax.ShapeDtypeStruct((width, levels), jnp.bfloat16),
        ),
        in_specs=[pl.BlockSpec(memory_space=pltpu.SMEM)]
        + [pl.BlockSpec(memory_space=pltpu.VMEM)] * 2,
        scratch_shapes=[
            pltpu.VMEM((width, levels), jnp.float32),
            pltpu.VMEM((members * rows, width), jnp.bfloat16),
            pltpu.VMEM((members // 2, width, 2 * LANES), jnp.bfloat16),
            pltpu.VMEM((members, members * rows, LANES), jnp.float32),
            pltpu.VMEM((members * rows, LANES), jnp.float32),
            pltpu.VMEM((members * rows, LANES), jnp.float32),
            pltpu.VMEM((members * rows, LANES), jnp.float32),
            pltpu.VMEM((16 * books, LANES), jnp.float32),
            pltpu.VMEM((levels // LANES, 16 * books, LANES), jnp.float32),
        ],
        name="core",
    )(me, group, codebooks.transpose(1, 0, 2).reshape(width, levels))
    part = lax.all_to_all(book_part.reshape(plane, -1, levels), PLANE, 0, 0)
    part = jnp.sum(part.astype(jnp.float32), axis=0).astype(jnp.bfloat16)
    part = spread(part, "ring")
    part = jnp.sum(part.astype(jnp.float32), axis=0).astype(jnp.bfloat16)
    part = spread(part, PLANE).astype(jnp.float32)
    book_total = part.reshape(sub_width, books, levels).transpose(1, 0, 2)
    return loss.reshape(rows), grad_queries, book_total


def solution(mesh):
    lines, stacks = mesh.devices.shape
    fine = Mesh(mesh.devices.reshape(lines, 2, stacks // 2), WHOLE)
    return jax.shard_map(
        per_device,
        mesh=fine,
        in_specs=(P(WHOLE, None), P(WHOLE, None), P(), P(WHOLE), P(WHOLE)),
        out_specs=(P(WHOLE), P(WHOLE, None), P()),
        check_vma=False,
    )
```

time: 181 us -> 97.1 us (0.54)
  blocking collectives: 159 us -> 57.5 us
  waiting for transfers between devices: 0 us -> 13.6 us
  starting transfers between devices: 0 us -> 10.2 us
  local copies, waits for them, and re-layouts: 5.01 us -> 0.9 us
  Pallas kernels: 16 us -> 12.8 us
    all_gather x3 -> x0, blocking collectives: 113 us -> none  [the longest x1 45 us: per_device(): part = lax.all_gather(part, 'pb', axis=0)]
    all_to_all x0 -> x1, waiting for transfers between devices: none -> 13.6 us  [per_device(): group = lax.all_to_all(pack, 'db', 0, 0)]
    all_to_all x2 -> x3, blocking collectives: 45.7 us -> 57.5 us  [the longest x2 43 us: spread(): return lax.all_to_all(copies, axis, 0, 0)]
    all_to_all x0 -> x1, starting transfers between devices: none -> 10.2 us  [per_device(): group = lax.all_to_all(pack, 'db', 0, 0)]
    pallas_call x2, Pallas kernels: 16 us -> 12.8 us  [the longest x1 10.8 us: per_device(): pl.pallas_call(functools.partial(main_kernel, scale, books), out_shape=(j...]
    unnamed x4 -> x2, local copies, waits for them, and re-layouts: 4.04 us -> 0.86 us
  transfers between devices with their start and end apart: 0 -> 1, of which waited for: 0 -> 1; matrix products, arithmetic and copies ran while one was open for 0% -> 0% of each run, Pallas kernels for 0% -> 0%
where the time goes in v3:
time: 97.1 us; the launch traced here: 96.7 us
  blocking collectives  57.5 us (59%)
  waiting for transfers between devices  13.6 us (14%)
  Pallas kernels  12.8 us (13%)
  starting transfers between devices  10.2 us (11%)
  other arithmetic  1.07 us (1%)
    all_to_all x2, blocking collectives, spread(): return lax.all_to_all(copies, axis, 0, 0)  43 us
    all_to_all x1, blocking collectives, per_device(): part = lax.all_to_all(book_part.reshape(plane, -1, levels), PLANE, 0, 0)  14.5 us
    all_to_all x1, waiting for transfers between devices, per_device(): group = lax.all_to_all(pack, 'db', 0, 0)  13.6 us
    pallas_call x1, Pallas kernels, per_device(): pl.pallas_call(functools.partial(main_kernel, scale, books), out_shape=(j...  10.8 us
    all_to_all x1, starting transfers between devices, per_device(): group = lax.all_to_all(pack, 'db', 0, 0)  10.2 us
  transfers between devices with their start and end apart: 1, of which 1 were waited for; matrix products, arithmetic and copies ran while one was open for 0% of the time, Pallas kernels for 0%

profile of v3, /device:TPU:1, one launch (start us, length us, event | category | flops | bytes accessed | tf_op | source)
XLA Modules:
  0.0 96.7 jit_solution(8853793165763392636)
XLA Ops:
  0.6 1.9 %pack.1 = bf16[16,176,128]{2,1,0:T(8,128)(2,1)} custom-call(bf16[16,768]{1,0:T(8,128)(2,1)} %queries_ref.1, s32[64,128]{1,0:T(8,128)} %bitcast.16, f32[1,16]{1,0:T(1,128)} %bitcast.17, s32[1,16]{1,0:T(1,128)} %bitcast.18), custom_call_target="tpu_custom_call" | custom-call | tf_op jit(solution)/shard_map/pack/pallas_call | solution.py:226
  2.6 10.2 %all-to-all-start = ((bf16[16,176,128]{2,1,0:T(8,128)(2,1)}), bf16[16,176,128]{2,1,0:T(8,128)(2,1)S(1)}, u32[]{:S(2)}, u32[]{:S(2)}) async-start(bf16[16,176,128]{2,1,0:T(8,128)(2,1)} %pack.1), calls=%async_computation | async-start | bytes 1441792 | tf_op jit(solution)/shard_map/all_to_all | solution.py:231
  12.8 13.6 %all-to-all-done.group_ref = bf16[16,176,128]{2,1,0:T(8,128)(2,1)S(1)} async-done(((bf16[16,176,128]{2,1,0:T(8,128)(2,1)}), bf16[16,176,128]{2,1,0:T(8,128)(2,1)S(1)}, u32[]{:S(2)}, u32[]{:S(2)}) %all-to-all-start) | async-done | bytes 720928 | tf_op jit(solution)/shard_map/all_to_all | solution.py:231
  26.4 0.0 copy-start
  26.4 0.9 copy-done
  27.2 10.8 %core.1 = (f32[1,16]{1,0:T(1,128)}, f32[16,768]{1,0:T(8,128)}, bf16[768,256]{1,0:T(8,128)(2,1)}) custom-call(s32[1,1]{1,0:T(1,128)} %bitcast.me_ref, bf16[16,176,128]{2,1,0:T(8,128)(2,1)} %copy-done, bf16[768,256]{1,0:T(8,128)(2,1)} %bitcast.15), custom_call_target="tpu_custom_call" | custom-call | tf_op jit(solution)/shard_map/core/pallas_call | solution.py:233
  38.1 14.5 %all_to_all.20 = bf16[32,24,256]{2,1,0:T(8,128)(2,1)S(1)} all-to-all(bf16[32,24,256]{2,1,0:T(8,128)(2,1)} %bitcast.14), channel_id=1, replica_groups=mesh['db'=16,'near'=2,'ring'=16] {'db','near'}, dimensions={0} | all-to-all | bytes 786432 | tf_op jit(solution)/shard_map/all_to_all | solution.py:255
  52.6 0.1 reduce_sum.24
  52.7 25.1 %all_to_all.21 = bf16[16,24,256]{2,1,0:T(8,128)(2,1)S(1)} all-to-all(bf16[16,24,256]{2,1,0:T(8,128)(2,1)S(1)} %broadcast_in_dim.4), channel_id=1, replica_groups=mesh['db'=16,'near'=2,'ring'=16] {'ring'}, dimensions={0} | all-to-all | bytes 393216 | tf_op jit(solution)/shard_map/all_to_all | solution.py:215
  77.9 17.8 %all_to_all.22 = bf16[32,24,256]{2,1,0:T(8,128)(2,1)S(1)} all-to-all(bf16[32,24,256]{2,1,0:T(8,128)(2,1)S(1)} %broadcast_in_dim.5), channel_id=1, replica_groups=mesh['db'=16,'near'=2,'ring'=16] {'db','near'}, dimensions={0} | all-to-all | bytes 786432 | tf_op jit(solution)/shard_map/all_to_all | solution.py:215
  95.7 1.0 convert_bitcast_fusion
  (3 shorter events, 0.1 us)
Async XLA Ops:
  2.6 23.8 %all-to-all-start = ((bf16[16,176,128]{2,1,0:T(8,128)(2,1)}), bf16[16,176,128]{2,1,0:T(8,128)(2,1)S(1)}, u32[]{:S(2)}, u32[]{:S(2)}) async-start(bf16[16,176,128]{2,1,0:T(8,128)(2,1)} %pack.1), calls=%async_computation | async-start | bytes 1441792 | tf_op jit(solution)/shard_map/all_to_all | solution.py:231
  26.4 0.9 copy-start

commit v4 on v3

v4 whole, which is shorter than its diff:
```python
import functools
import math

import jax
import jax.numpy as jnp
from jax import lax
from jax.experimental import pallas as pl
from jax.experimental.pallas import tpu as pltpu
from jax.sharding import Mesh
from jax.sharding import PartitionSpec as P

LANES = 128
PLANE = ("db", "near", "pair")
WHOLE = ("db", "near", "far", "pair")


def order_table(width, books, inverse):
    sub_width = width // books
    row = lax.broadcasted_iota(jnp.int32, (width, 1 if inverse else width), 0)
    column = lax.broadcasted_iota(jnp.int32, (width if inverse else 1, width), 1)
    place = row if inverse else column
    inner = place % (8 * sub_width)
    source = (place // (8 * sub_width) * 8 + inner % 8) * sub_width + inner // 8
    other = column if inverse else row
    return jnp.where(other == source, 1.0, 0.0).astype(jnp.bfloat16)


def pack_kernel(queries_ref, codes_ref, weight_ref, positive_ref, out_ref):
    rows, width = queries_ref.shape
    books = codes_ref.shape[0]
    top = rows * (width // LANES)
    code_rows = codes_ref[...].astype(jnp.float32).astype(jnp.bfloat16)
    spot = lax.broadcasted_iota(jnp.int32, (rows, rows), 0)
    lane = lax.broadcasted_iota(jnp.int32, (rows, rows), 1)

    def column(row):
        spread_row = jnp.broadcast_to(row, (rows, rows))
        return jnp.sum(jnp.where(spot == lane, spread_row, 0.0), axis=1, keepdims=True)

    weight = column(weight_ref[...])
    positive = positive_ref[...]
    first = weight.astype(jnp.bfloat16).astype(jnp.float32)
    second = (weight - first).astype(jnp.bfloat16).astype(jnp.float32)
    third = weight - first - second
    block = column((positive // LANES).astype(jnp.float32))
    place = column((positive % LANES).astype(jnp.float32))
    wide = lax.broadcasted_iota(jnp.int32, (rows, LANES), 1)
    extra = jnp.zeros((rows, LANES), jnp.float32)
    for j, value in enumerate((first, second, third, block, place)):
        extra = jnp.where(wide == j, value, extra)
    extra = extra.astype(jnp.bfloat16)
    for d in range(out_ref.shape[0]):
        for j in range(width // LANES):
            out_ref[d, rows * j : rows * (j + 1), :] = queries_ref[
                :, LANES * j : LANES * (j + 1)
            ]
        out_ref[d, top : top + books, :] = code_rows
        out_ref[d, top + books :, :] = extra


def main_kernel(
    scale, books, me_ref, group_ref, cb_ref,
    loss_ref, gq_ref, gb_ref,
    cb_scr, q_scr, sorted_scr, dec_scr, s_scr, max_scr, sum_scr, total_scr, pg_scr,
):
    members = group_ref.shape[0]
    width, levels = cb_ref.shape
    sub_width = width // books
    rows = gq_ref.shape[0]
    blocks = width // LANES
    top = rows * blocks
    queries = members * rows
    me = me_ref[0, 0]
    cb_scr[...] = cb_ref[...].astype(jnp.float32)
    for j in range(blocks):
        q_scr[:, LANES * j : LANES * (j + 1)] = group_ref[
            :, rows * j : rows * (j + 1), :
        ].reshape(queries, LANES)
    sorted_scr[...] = jnp.dot(
        q_scr[...], order_table(width, books, False), preferred_element_type=jnp.float32
    ).astype(jnp.bfloat16)

    def decode(t):
        for side in range(2):
            codes = (
                group_ref[2 * t + side, top : top + books, :]
                .astype(jnp.float32)
                .astype(jnp.int32)
            )
            for g in range(books // 8):
                index = codes[8 * g : 8 * g + 8, :]
                inner = index & (LANES - 1)
                upper = index >= LANES
                for two in range(sub_width // 2):
                    tiles = []
                    for c in (2 * two, 2 * two + 1):
                        at = c * books + 8 * g
                        low = jnp.take_along_axis(cb_scr[at : at + 8, :LANES], inner, axis=1)
                        high = jnp.take_along_axis(cb_scr[at : at + 8, LANES:], inner, axis=1)
                        tiles.append(jnp.where(upper, high, low))
                    at = 8 * sub_width * g + 16 * two
                    dec_scr[t, at : at + 16, LANES * side : LANES * side + LANES] = (
                        jnp.concatenate(tiles, axis=0).astype(jnp.bfloat16)
                    )

    def score(t):
        both = jnp.dot(sorted_scr[...], dec_scr[t], preferred_element_type=jnp.float32)
        for r in range(0, queries, 32):
            left = both[r : r + 32, :LANES] * scale
            right = both[r : r + 32, LANES:] * scale
            s_scr[2 * t, r : r + 32, :] = left
            s_scr[2 * t + 1, r : r + 32, :] = right
            newest = jnp.maximum(left, right)
            if t > 0:
                before = max_scr[r : r + 32, :]
                newest = jnp.maximum(newest, before)
            total = jnp.exp(left - newest) + jnp.exp(right - newest)
            if t > 0:
                total = total + sum_scr[r : r + 32, :] * jnp.exp(before - newest)
            max_scr[r : r + 32, :] = newest
            sum_scr[r : r + 32, :] = total

    for t in range(members // 2):
        decode(t)
        score(t)

    highest = max_scr[...]
    row_max = jnp.max(highest, axis=1, keepdims=True)
    total = jnp.sum(sum_scr[...] * jnp.exp(highest - row_max), axis=1, keepdims=True)
    total_scr[...] = jnp.broadcast_to(row_max + jnp.log(total), (queries, LANES))

    def extras(block):
        weight = block[:, 0:1] + block[:, 1:2] + block[:, 2:3]
        return weight, block[:, 3:4], block[:, 4:5]

    extra = group_ref[:, top + books :, :].reshape(queries, LANES).astype(jnp.float32)
    weight, block, place = extras(extra)
    here = me.astype(jnp.float32)
    lane = lax.broadcasted_iota(jnp.int32, (queries, LANES), 1).astype(jnp.float32)
    is_positive = jnp.where((block == here) & (place == lane), 1.0, 0.0)
    coefficient = (
        weight * (jnp.exp(s_scr[me] - total_scr[...]) - is_positive) * scale
    ).astype(jnp.bfloat16)
    pg_scr[...] = lax.dot_general(
        q_scr[...], coefficient, (((0,), (0,)), ((), ())), preferred_element_type=jnp.float32
    )

    own_codes = group_ref[me, top : top + books, :].astype(jnp.float32)
    level = lax.broadcasted_iota(jnp.int32, (levels, LANES), 0).astype(jnp.float32)
    level = level.astype(jnp.bfloat16)
    one = jnp.ones((16, LANES), jnp.bfloat16)
    zero = jnp.zeros((16, LANES), jnp.bfloat16)
    pair_rows = 2 * sub_width
    upper = lax.broadcasted_iota(jnp.int32, (pair_rows, LANES), 0) < sub_width
    ready = []
    for m in range(0, books, 2):
        tables = []
        for h in range(2):
            row = jnp.broadcast_to(own_codes[m + h : m + h + 1, :], (16, LANES)).astype(
                jnp.bfloat16
            )
            tables.append(
                jnp.concatenate(
                    [
                        jnp.where(row == level[16 * j : 16 * j + 16, :], one, zero)
                        for j in range(levels // 16)
                    ],
                    axis=0,
                )
            )
        terms = pg_scr[sub_width * m : sub_width * m + pair_rows, :]
        high = terms.astype(jnp.bfloat16).astype(jnp.float32)
        parts = [
            jnp.concatenate([jnp.where(upper, x, 0.0), jnp.where(upper, 0.0, x)], axis=1)
            for x in (high, terms - high)
        ]
        sums = lax.dot_general(
            jnp.concatenate(parts, axis=0).astype(jnp.bfloat16),
            jnp.concatenate(tables, axis=1),
            (((1,), (1,)), ((), ())),
            preferred_element_type=jnp.float32,
        )
        ready.append(sums[:pair_rows] + sums[pair_rows:])
        if m % 4 == 2:
            at = sub_width * (m - 2)
            both = jnp.concatenate(ready, axis=0).astype(jnp.bfloat16)
            for j in range(levels // LANES):
                gb_ref[j, at : at + 2 * pair_rows, :] = both[:, LANES * j : LANES * (j + 1)]
            ready = []

    own = pl.ds(pl.multiple_of(me * rows, rows), rows)
    weight, block, place = extras(group_ref[me, top + books :, :].astype(jnp.float32))
    own_total = total_scr[own, :]
    own_lane = lax.broadcasted_iota(jnp.int32, (rows, LANES), 1).astype(jnp.float32)
    chosen = jnp.zeros((rows, LANES), jnp.float32)
    grad = jnp.zeros((rows, width), jnp.float32)
    for t in range(members // 2):
        parts = []
        for d in (2 * t, 2 * t + 1):
            scores = s_scr[d, own, :]
            hit = (block == float(d)) & (place == own_lane)
            chosen = chosen + jnp.where(hit, scores, 0.0)
            parts.append(
                weight * (jnp.exp(scores - own_total) - jnp.where(hit, 1.0, 0.0)) * scale
            )
        grad = grad + lax.dot_general(
            jnp.concatenate(parts, axis=1).astype(jnp.bfloat16),
            dec_scr[t],
            (((1,), (1,)), ((), ())),
            preferred_element_type=jnp.float32,
        )
    gq_ref[...] = grad
    loss = weight * (own_total - jnp.sum(chosen, axis=1, keepdims=True))
    diagonal = lax.broadcasted_iota(jnp.int32, (rows, LANES), 0).astype(jnp.float32) == own_lane
    loss_ref[...] = jnp.sum(jnp.where(diagonal, loss, 0.0), axis=0, keepdims=True)[:, :rows]


def restore_kernel(books, grad_ref, out_ref):
    rows, width = grad_ref.shape
    grad = grad_ref[...]
    first = grad.astype(jnp.bfloat16).astype(jnp.float32)
    second = (grad - first).astype(jnp.bfloat16).astype(jnp.float32)
    third = grad - first - second
    restored = jnp.dot(
        jnp.concatenate([first, second, third], axis=0).astype(jnp.bfloat16),
        order_table(width, books, True),
        preferred_element_type=jnp.float32,
    )
    out_ref[...] = restored[:rows] + restored[rows : 2 * rows] + restored[2 * rows :]


def spread(block, axis):
    copies = jnp.broadcast_to(block[None], (lax.axis_size(axis),) + block.shape)
    return lax.all_to_all(copies, axis, 0, 0)


def per_device(queries, passage_codes, codebooks, positives, loss_weight):
    rows, width = queries.shape
    books = passage_codes.shape[1]
    sub_width, levels = codebooks.shape[1:]
    members = lax.axis_size("db")
    plane = lax.axis_size(PLANE)
    pack_rows = rows * (width // LANES) + books + rows
    scale = 2.5 / math.sqrt(width)
    pack = pl.pallas_call(
        pack_kernel,
        out_shape=jax.ShapeDtypeStruct((members, pack_rows, LANES), jnp.bfloat16),
        compiler_params=pltpu.CompilerParams(vmem_limit_bytes=8 * 1024 * 1024),
        name="pack",
    )(queries, passage_codes.T, loss_weight.reshape(1, rows), positives.reshape(1, rows))
    group = lax.all_to_all(pack, "db", 0, 0)
    me = lax.axis_index("db").astype(jnp.int32).reshape(1, 1)
    loss, grad_queries, book_part = pl.pallas_call(
        functools.partial(main_kernel, scale, books),
        out_shape=(
            jax.ShapeDtypeStruct((1, rows), jnp.float32),
            jax.ShapeDtypeStruct((rows, width), jnp.float32),
            jax.ShapeDtypeStruct((levels // LANES, width, LANES), jnp.bfloat16),
        ),
        in_specs=[pl.BlockSpec(memory_space=pltpu.SMEM)]
        + [pl.BlockSpec(memory_space=pltpu.VMEM)] * 2,
        scratch_shapes=[
            pltpu.VMEM((width, levels), jnp.float32),
            pltpu.VMEM((members * rows, width), jnp.bfloat16),
            pltpu.VMEM((members * rows, width), jnp.bfloat16),
            pltpu.VMEM((members // 2, width, 2 * LANES), jnp.bfloat16),
            pltpu.VMEM((members, members * rows, LANES), jnp.float32),
            pltpu.VMEM((members * rows, LANES), jnp.float32),
            pltpu.VMEM((members * rows, LANES), jnp.float32),
            pltpu.VMEM((members * rows, LANES), jnp.float32),
            pltpu.VMEM((width, LANES), jnp.float32),
        ],
        compiler_params=pltpu.CompilerParams(vmem_limit_bytes=24 * 1024 * 1024),
        name="core",
    )(me, group, codebooks.transpose(1, 0, 2).reshape(width, levels))
    grad_queries = pl.pallas_call(
        functools.partial(restore_kernel, books),
        out_shape=jax.ShapeDtypeStruct((rows, width), jnp.float32),
        compiler_params=pltpu.CompilerParams(vmem_limit_bytes=8 * 1024 * 1024),
        name="restore",
    )(grad_queries)
    part = lax.all_to_all(book_part.reshape(plane, -1, LANES), PLANE, 0, 0)
    part = jnp.sum(part.astype(jnp.float32), axis=0).astype(jnp.bfloat16)
    part = spread(part, "far")
    part = jnp.sum(part.astype(jnp.float32), axis=0).astype(jnp.bfloat16)
    part = spread(part, PLANE).astype(jnp.float32)
    book_total = part.reshape(-1, books, sub_width, LANES).transpose(1, 2, 0, 3)
    return loss.reshape(rows), grad_queries, book_total.reshape(books, sub_width, levels)


def solution(mesh):
    lines, stacks = mesh.devices.shape
    fine = Mesh(mesh.devices.reshape(lines, 2, stacks // 4, 2), WHOLE)
    return jax.shard_map(
        per_device,
        mesh=fine,
        in_specs=(P(WHOLE, None), P(WHOLE, None), P(), P(WHOLE), P(WHOLE)),
        out_specs=(P(WHOLE), P(WHOLE, None), P()),
        check_vma=False,
    )
```

time: 97.1 us -> 95.7 us (0.986)
  blocking collectives: 57.5 us -> 40.3 us
  waiting for transfers between devices: 13.6 us -> 23.6 us
  starting transfers between devices: 10.2 us -> 16.4 us
  local copies, waits for them, and re-layouts: 0.9 us -> 5.15 us
  Pallas kernels: 12.8 us -> 8.95 us
    all_to_all x2 -> x1, blocking collectives: 43 us -> 24.6 us  [spread(): return lax.all_to_all(copies, axis, 0, 0)]
    all_to_all x0 -> x1, waiting for transfers between devices: none -> 10 us  [spread(): return lax.all_to_all(copies, axis, 0, 0)]
    all_to_all x0 -> x1, starting transfers between devices: none -> 6.03 us  [spread(): return lax.all_to_all(copies, axis, 0, 0)]
    pallas_call x1, Pallas kernels: 10.8 us -> 6.6 us  [per_device(): pl.pallas_call(functools.partial(main_kernel, scale, books), out_shape=(j...]
    reshape x0 -> x3, local copies, waits for them, and re-layouts: none -> 2.19 us  [per_device(): book_total.reshape(books, sub_width, levels)]
    pallas_call x0 -> x1, Pallas kernels: none -> 1.4 us  [per_device(): pl.pallas_call(functools.partial(restore_kernel, books), out_shape=jax.Sh...]
    unnamed x2 -> x10, local copies, waits for them, and re-layouts: 0.86 us -> 2.15 us
    all_to_all x1, blocking collectives: 14.5 us -> 15.8 us  [per_device(): part = lax.all_to_all(book_part.reshape(plane, -1, LANES), PLANE, 0, 0)]
  transfers between devices with their start and end apart: 1 -> 2, of which waited for: 1 -> 2; matrix products, arithmetic and copies ran while one was open for 0% -> 0% of each run, Pallas kernels for 0% -> 1%
where the time goes in v4:
time: 95.7 us; the launch traced here: 95.2 us
  blocking collectives  40.3 us (42%)
  waiting for transfers between devices  23.6 us (25%)
  starting transfers between devices  16.4 us (17%)
  Pallas kernels  8.95 us (9%)
  local copies, waits for them, and re-layouts  5.15 us (5%)
    all_to_all x1, blocking collectives, spread(): return lax.all_to_all(copies, axis, 0, 0)  24.6 us
    all_to_all x1, blocking collectives, per_device(): part = lax.all_to_all(book_part.reshape(plane, -1, LANES), PLANE, 0, 0)  15.8 us
    all_to_all x1, waiting for transfers between devices, per_device(): group = lax.all_to_all(pack, 'db', 0, 0)  13.6 us
    all_to_all x1, starting transfers between devices, per_device(): group = lax.all_to_all(pack, 'db', 0, 0)  10.4 us
    all_to_all x1, waiting for transfers between devices, spread(): return lax.all_to_all(copies, axis, 0, 0)  10 us
    pallas_call x1, Pallas kernels, per_device(): pl.pallas_call(functools.partial(main_kernel, scale, books), out_shape=(j...  6.6 us
    all_to_all x1, starting transfers between devices, spread(): return lax.all_to_all(copies, axis, 0, 0)  6.03 us
    reshape x3, local copies, waits for them, and re-layouts, per_device(): book_total.reshape(books, sub_width, levels)  2.19 us
  transfers between devices with their start and end apart: 2, of which 2 were waited for; matrix products, arithmetic and copies ran while one was open for 0% of the time, Pallas kernels for 1%

profile of v4, /device:TPU:1, one launch (start us, length us, event | category | flops | bytes accessed | tf_op | source)
XLA Modules:
  0.0 95.2 jit_solution(11200530148051626739)
XLA Ops:
  0.6 0.0 copy-start.3
  0.6 0.0 copy-start.4
  0.7 0.6 copy-done.3
  1.3 0.0 copy-done.4
  1.3 0.0 copy-start.1
  1.3 0.8 copy-done.1
  2.1 0.0 copy-start.2
  2.1 0.7 copy-done.2
  2.8 1.0 %pack.1 = bf16[16,176,128]{2,1,0:T(8,128)(2,1)} custom-call(bf16[16,768]{1,0:T(8,128)(2,1)S(1)} %copy-done.2, s32[64,128]{1,0:T(8,128)S(1)} %bitcast.14, f32[1,16]{1,0:T(1,128)S(1)} %bitcast.15, s32[1,16]{1,0:T(1,128)S(1)} %bitcast.16), custom_call_target="tpu_custom_call" | custom-call | tf_op jit(solution)/shard_map/pack/pallas_call | solution.py:245
  3.8 0.0 copy-start
  3.8 10.4 %all-to-all-start = ((bf16[16,176,128]{2,1,0:T(8,128)(2,1)}), bf16[16,176,128]{2,1,0:T(8,128)(2,1)S(1)}, u32[]{:S(2)}, u32[]{:S(2)}) async-start(bf16[16,176,128]{2,1,0:T(8,128)(2,1)} %pack.1), calls=%async_computation | async-start | bytes 1441792 | tf_op jit(solution)/shard_map/all_to_all | solution.py:251
  14.1 13.6 %all-to-all-done.group_ref = bf16[16,176,128]{2,1,0:T(8,128)(2,1)S(1)} async-done(((bf16[16,176,128]{2,1,0:T(8,128)(2,1)}), bf16[16,176,128]{2,1,0:T(8,128)(2,1)S(1)}, u32[]{:S(2)}, u32[]{:S(2)}) %all-to-all-start) | async-done | bytes 720928 | tf_op jit(solution)/shard_map/all_to_all | solution.py:251
  27.7 0.0 copy-done
  27.7 6.6 %core.1 = (f32[1,16]{1,0:T(1,128)}, f32[16,768]{1,0:T(8,128)S(1)}, bf16[2,768,128]{2,1,0:T(8,128)(2,1)S(1)}) custom-call(s32[1,1]{1,0:T(1,128)} %bitcast.me_ref, bf16[16,176,128]{2,1,0:T(8,128)(2,1)S(1)} %all-to-all-done.group_ref, bf16[768,256]{1,0:T(8,128)(2,1)S(1)} %bitcast.13), custom_call_target="tpu_custom_call" | custom-call | tf_op jit(solution)/shard_map/core/pallas_call | solution.py:253
  34.3 15.8 %all_to_all.20 = bf16[64,24,128]{2,1,0:T(8,128)(2,1)S(1)} all-to-all(bf16[64,24,128]{2,1,0:T(8,128)(2,1)S(1)} %bitcast.12), channel_id=1, replica_groups=mesh['db'=16,'near'=2,'far'=8,'pair'=2] {'db','near','pair'}, dimensions={0} | all-to-all | bytes 786432 | tf_op jit(solution)/shard_map/all_to_all | solution.py:282
  50.1 0.1 reduce_sum.24
  50.2 24.6 %all_to_all.21 = bf16[8,24,128]{2,1,0:T(8,128)(2,1)S(1)} all-to-all(bf16[8,24,128]{2,1,0:T(8,128)(2,1)S(1)} %broadcast_in_dim.4), channel_id=1, replica_groups=mesh['db'=16,'near'=2,'far'=8,'pair'=2] {'far'}, dimensions={0} | all-to-all | bytes 98304 | tf_op jit(solution)/shard_map/all_to_all | solution.py:234
  74.7 0.8 broadcast_in_dim.5
  75.5 6.0 %all-to-all-start.3 = ((bf16[64,24,128]{2,1,0:T(8,128)(2,1)}), bf16[64,24,128]{2,1,0:T(8,128)(2,1)S(1)}, u32[]{:S(2)}, u32[]{:S(2)}) async-start(bf16[64,24,128]{2,1,0:T(8,128)(2,1)} %broadcast_in_dim.5), calls=%async_computation.3 | async-start | bytes 786432 | tf_op jit(solution)/shard_map/all_to_all | solution.py:234
  81.6 1.4 %restore.1 = f32[16,768]{1,0:T(8,128)} custom-call(f32[16,768]{1,0:T(8,128)S(1)} %get-tuple-element.7.grad_ref), custom_call_target="tpu_custom_call" | custom-call | tf_op jit(solution)/shard_map/restore/pallas_call | solution.py:276
  83.0 10.0 %all-to-all-done.3 = bf16[64,24,128]{2,1,0:T(8,128)(2,1)S(1)} async-done(((bf16[64,24,128]{2,1,0:T(8,128)(2,1)}), bf16[64,24,128]{2,1,0:T(8,128)(2,1)S(1)}, u32[]{:S(2)}, u32[]{:S(2)}) %all-to-all-start.3) | async-done | bytes 393248 | tf_op jit(solution)/shard_map/all_to_all | solution.py:234
  93.0 0.1 reshape.49
  93.1 0.6 copy.9
  93.7 1.5 %reshape.46 = f32[64,12,256]{2,0,1:T(8,128)} reshape(f32[64,12,2,128]{3,2,0,1:T(2,128)S(1)} %copy.9) | data formatting | bytes 1572864 | tf_op jit(solution)/shard_map/reshape | solution.py:288
  (2 shorter events, 0.0 us)
Async XLA Ops:
  0.6 0.7 copy-start.3
  0.6 0.7 copy-start.4
  1.3 0.8 copy-start.1
  2.1 0.7 copy-start.2
  3.8 24.0 %copy-start = (bf16[64,12,256]{2,0,1:T(8,128)(2,1)S(1)}, bf16[64,12,256]{2,0,1:T(8,128)(2,1)}, u32[]{:S(2)}) copy-start(bf16[64,12,256]{2,0,1:T(8,128)(2,1)} %param.7) | copy-start | bytes 1179652
  3.8 24.0 %all-to-all-start = ((bf16[16,176,128]{2,1,0:T(8,128)(2,1)}), bf16[16,176,128]{2,1,0:T(8,128)(2,1)S(1)}, u32[]{:S(2)}, u32[]{:S(2)}) async-start(bf16[16,176,128]{2,1,0:T(8,128)(2,1)} %pack.1), calls=%async_computation | async-start | bytes 1441792 | tf_op jit(solution)/shard_map/all_to_all | solution.py:251
  75.5 17.5 %all-to-all-start.3 = ((bf16[64,24,128]{2,1,0:T(8,128)(2,1)}), bf16[64,24,128]{2,1,0:T(8,128)(2,1)S(1)}, u32[]{:S(2)}, u32[]{:S(2)}) async-start(bf16[64,24,128]{2,1,0:T(8,128)(2,1)} %broadcast_in_dim.5), calls=%async_computation.3 | async-start | bytes 786432 | tf_op jit(solution)/shard_map/all_to_all | solution.py:234

commit v5 on v4

--- a/solution.py
+++ b/solution.py
@@ -14,15 +14,13 @@
 WHOLE = ("db", "near", "far", "pair")
 
 
-def order_table(width, books, inverse):
+def order_table(width, books):
     sub_width = width // books
-    row = lax.broadcasted_iota(jnp.int32, (width, 1 if inverse else width), 0)
-    column = lax.broadcasted_iota(jnp.int32, (width if inverse else 1, width), 1)
-    place = row if inverse else column
+    row = lax.broadcasted_iota(jnp.int32, (width, width), 0)
+    place = lax.broadcasted_iota(jnp.int32, (1, width), 1)
     inner = place % (8 * sub_width)
     source = (place // (8 * sub_width) * 8 + inner % 8) * sub_width + inner // 8
-    other = column if inverse else row
-    return jnp.where(other == source, 1.0, 0.0).astype(jnp.bfloat16)
+    return jnp.where(row == source, 1.0, 0.0).astype(jnp.bfloat16)
 
 
 def pack_kernel(queries_ref, codes_ref, weight_ref, positive_ref, out_ref):
@@ -61,7 +59,7 @@
 def main_kernel(
     scale, books, me_ref, group_ref, cb_ref,
     loss_ref, gq_ref, gb_ref,
-    cb_scr, q_scr, sorted_scr, dec_scr, s_scr, max_scr, sum_scr, total_scr, pg_scr,
+    cb_scr, q_scr, table_scr, sorted_scr, dec_scr, s_scr, max_scr, sum_scr, total_scr, pg_scr,
 ):
     members = group_ref.shape[0]
     width, levels = cb_ref.shape
@@ -76,8 +74,9 @@
         q_scr[:, LANES * j : LANES * (j + 1)] = group_ref[
             :, rows * j : rows * (j + 1), :
         ].reshape(queries, LANES)
+    table_scr[...] = order_table(width, books)
     sorted_scr[...] = jnp.dot(
-        q_scr[...], order_table(width, books, False), preferred_element_type=jnp.float32
+        q_scr[...], table_scr[...], preferred_element_type=jnp.float32
     ).astype(jnp.bfloat16)
 
     def decode(t):
@@ -142,23 +141,28 @@
         weight * (jnp.exp(s_scr[me] - total_scr[...]) - is_positive) * scale
     ).astype(jnp.bfloat16)
     pg_scr[...] = lax.dot_general(
-        q_scr[...], coefficient, (((0,), (0,)), ((), ())), preferred_element_type=jnp.float32
-    )
+        sorted_scr[...],
+        coefficient,
+        (((0,), (0,)), ((), ())),
+        preferred_element_type=jnp.float32,
+    ).astype(jnp.bfloat16)
 
     own_codes = group_ref[me, top : top + books, :].astype(jnp.float32)
     level = lax.broadcasted_iota(jnp.int32, (levels, LANES), 0).astype(jnp.float32)
     level = level.astype(jnp.bfloat16)
     one = jnp.ones((16, LANES), jnp.bfloat16)
     zero = jnp.zeros((16, LANES), jnp.bfloat16)
-    pair_rows = 2 * sub_width
-    upper = lax.broadcasted_iota(jnp.int32, (pair_rows, LANES), 0) < sub_width
-    ready = []
-    for m in range(0, books, 2):
+    part_rows = 8 * sub_width
+    spot = lax.broadcasted_iota(jnp.int32, (part_rows, LANES), 0) % 8
+    spot = spot.astype(jnp.float32).astype(jnp.bfloat16)
+    blank = jnp.zeros((part_rows, LANES), jnp.bfloat16)
+    for g in range(books // 8):
         tables = []
-        for h in range(2):
-            row = jnp.broadcast_to(own_codes[m + h : m + h + 1, :], (16, LANES)).astype(
-                jnp.bfloat16
-            )
+        parts = []
+        terms = pg_scr[part_rows * g : part_rows * (g + 1), :]
+        for i in range(8):
+            m = 8 * g + i
+            row = jnp.broadcast_to(own_codes[m : m + 1, :], (16, LANES)).astype(jnp.bfloat16)
             tables.append(
                 jnp.concatenate(
                     [
@@ -168,25 +172,17 @@
                     axis=0,
                 )
             )
-        terms = pg_scr[sub_width * m : sub_width * m + pair_rows, :]
-        high = terms.astype(jnp.bfloat16).astype(jnp.float32)
-        parts = [
-            jnp.concatenate([jnp.where(upper, x, 0.0), jnp.where(upper, 0.0, x)], axis=1)
-            for x in (high, terms - high)
-        ]
+            parts.append(jnp.where(spot == jnp.full_like(spot, i), terms, blank))
         sums = lax.dot_general(
-            jnp.concatenate(parts, axis=0).astype(jnp.bfloat16),
+            jnp.concatenate(parts, axis=1),
             jnp.concatenate(tables, axis=1),
             (((1,), (1,)), ((), ())),
             preferred_element_type=jnp.float32,
-        )
-        ready.append(sums[:pair_rows] + sums[pair_rows:])
-        if m % 4 == 2:
-            at = sub_width * (m - 2)
-            both = jnp.concatenate(ready, axis=0).astype(jnp.bfloat16)
+        ).astype(jnp.bfloat16)
+        for c in range(sub_width):
+            at = c * books + 8 * g
             for j in range(levels // LANES):
-                gb_ref[j, at : at + 2 * pair_rows, :] = both[:, LANES * j : LANES * (j + 1)]
-            ready = []
+                gb_ref[j, at : at + 8, :] = sums[8 * c : 8 * c + 8, LANES * j : LANES * (j + 1)]
 
     own = pl.ds(pl.multiple_of(me * rows, rows), rows)
     weight, block, place = extras(group_ref[me, top + books :, :].astype(jnp.float32))
@@ -209,24 +205,24 @@
             (((1,), (1,)), ((), ())),
             preferred_element_type=jnp.float32,
         )
-    gq_ref[...] = grad
+    first = grad.astype(jnp.bfloat16).astype(jnp.float32)
+    second = (grad - first).astype(jnp.bfloat16).astype(jnp.float32)
+    third = grad - first - second
+    restored = lax.dot_general(
+        jnp.concatenate([first, second, third], axis=0).astype(jnp.bfloat16),
+        table_scr[...],
+        (((1,), (1,)), ((), ())),
+        preferred_element_type=jnp.float32,
+    )
+    gq_ref[...] = restored[:rows] + restored[rows : 2 * rows] + restored[2 * rows :]
     loss = weight * (own_total - jnp.sum(chosen, axis=1, keepdims=True))
     diagonal = lax.broadcasted_iota(jnp.int32, (rows, LANES), 0).astype(jnp.float32) == own_lane
     loss_ref[...] = jnp.sum(jnp.where(diagonal, loss, 0.0), axis=0, keepdims=True)[:, :rows]
 
 
-def restore_kernel(books, grad_ref, out_ref):
-    rows, width = grad_ref.shape
-    grad = grad_ref[...]
-    first = grad.astype(jnp.bfloat16).astype(jnp.float32)
-    second = (grad - first).astype(jnp.bfloat16).astype(jnp.float32)
-    third = grad - first - second
-    restored = jnp.dot(
-        jnp.concatenate([first, second, third], axis=0).astype(jnp.bfloat16),
-        order_table(width, books, True),
-        preferred_element_type=jnp.float32,
-    )
-    out_ref[...] = restored[:rows] + restored[rows : 2 * rows] + restored[2 * rows :]
+def widen_kernel(part_ref, out_ref):
+    for j in range(part_ref.shape[0]):
+        out_ref[:, LANES * j : LANES * (j + 1)] = part_ref[j].astype(jnp.float32)
 
 
 def spread(block, axis):
@@ -245,7 +241,6 @@
     pack = pl.pallas_call(
         pack_kernel,
         out_shape=jax.ShapeDtypeStruct((members, pack_rows, LANES), jnp.bfloat16),
-        compiler_params=pltpu.CompilerParams(vmem_limit_bytes=8 * 1024 * 1024),
         name="pack",
     )(queries, passage_codes.T, loss_weight.reshape(1, rows), positives.reshape(1, rows))
     group = lax.all_to_all(pack, "db", 0, 0)
@@ -262,30 +257,31 @@
         scratch_shapes=[
             pltpu.VMEM((width, levels), jnp.float32),
             pltpu.VMEM((members * rows, width), jnp.bfloat16),
+            pltpu.VMEM((width, width), jnp.bfloat16),
             pltpu.VMEM((members * rows, width), jnp.bfloat16),
             pltpu.VMEM((members // 2, width, 2 * LANES), jnp.bfloat16),
             pltpu.VMEM((members, members * rows, LANES), jnp.float32),
             pltpu.VMEM((members * rows, LANES), jnp.float32),
             pltpu.VMEM((members * rows, LANES), jnp.float32),
             pltpu.VMEM((members * rows, LANES), jnp.float32),
-            pltpu.VMEM((width, LANES), jnp.float32),
+            pltpu.VMEM((width, LANES), jnp.bfloat16),
         ],
         compiler_params=pltpu.CompilerParams(vmem_limit_bytes=24 * 1024 * 1024),
         name="core",
     )(me, group, codebooks.transpose(1, 0, 2).reshape(width, levels))
-    grad_queries = pl.pallas_call(
-        functools.partial(restore_kernel, books),
-        out_shape=jax.ShapeDtypeStruct((rows, width), jnp.float32),
-        compiler_params=pltpu.CompilerParams(vmem_limit_bytes=8 * 1024 * 1024),
-        name="restore",
-    )(grad_queries)
     part = lax.all_to_all(book_part.reshape(plane, -1, LANES), PLANE, 0, 0)
     part = jnp.sum(part.astype(jnp.float32), axis=0).astype(jnp.bfloat16)
     part = spread(part, "far")
     part = jnp.sum(part.astype(jnp.float32), axis=0).astype(jnp.bfloat16)
-    part = spread(part, PLANE).astype(jnp.float32)
-    book_total = part.reshape(-1, books, sub_width, LANES).transpose(1, 2, 0, 3)
-    return loss.reshape(rows), grad_queries, book_total.reshape(books, sub_width, levels)
+    part = spread(part, PLANE).reshape(-1, width, LANES)
+    book_total = pl.pallas_call(
+        widen_kernel,
+        out_shape=jax.ShapeDtypeStruct((width, levels), jnp.float32),
+        compiler_params=pltpu.CompilerParams(vmem_limit_bytes=8 * 1024 * 1024),
+        name="widen",
+    )(part)
+    book_total = book_total.reshape(sub_width, books, levels).transpose(1, 0, 2)
+    return loss.reshape(rows), grad_queries, book_total
 
 
 def solution(mesh):

time: 95.7 us -> 93.3 us (0.975)
  blocking collectives: 40.3 us -> 57.2 us
  waiting for transfers between devices: 23.6 us -> 13.6 us
  starting transfers between devices: 16.4 us -> 10.4 us
  local copies, waits for them, and re-layouts: 5.15 us -> 0.07 us
  Pallas kernels: 8.95 us -> 11 us
    all_to_all x1 -> x2, blocking collectives: 24.6 us -> 41.4 us  [spread(): return lax.all_to_all(copies, axis, 0, 0)]
    all_to_all x1 -> x0, waiting for transfers between devices: 10 us -> none  [spread(): return lax.all_to_all(copies, axis, 0, 0)]
    all_to_all x1 -> x0, starting transfers between devices: 6.03 us -> none  [spread(): return lax.all_to_all(copies, axis, 0, 0)]
    reshape x3 -> x0, local copies, waits for them, and re-layouts: 2.19 us -> none  [per_device(): book_total.reshape(books, sub_width, levels)]
    unnamed x10 -> x2, local copies, waits for them, and re-layouts: 2.15 us -> 0.01 us
    pallas_call x1, Pallas kernels: 6.6 us -> 8.37 us  [per_device(): pl.pallas_call(functools.partial(main_kernel, scale, books), out_shape=(j...]
  transfers between devices with their start and end apart: 2 -> 1, of which waited for: 2 -> 1; matrix products, arithmetic and copies ran while one was open for 0% -> 0% of each run, Pallas kernels for 1% -> 0%
where the time goes in v5:
time: 93.3 us; the launch traced here: 93 us
  blocking collectives  57.2 us (61%)
  waiting for transfers between devices  13.6 us (15%)
  Pallas kernels  11 us (12%)
  starting transfers between devices  10.4 us (11%)
    all_to_all x2, blocking collectives, spread(): return lax.all_to_all(copies, axis, 0, 0)  41.4 us
    all_to_all x1, blocking collectives, per_device(): part = lax.all_to_all(book_part.reshape(plane, -1, LANES), PLANE, 0, 0)  15.7 us
    all_to_all x1, waiting for transfers between devices, per_device(): group = lax.all_to_all(pack, 'db', 0, 0)  13.6 us
    all_to_all x1, starting transfers between devices, per_device(): group = lax.all_to_all(pack, 'db', 0, 0)  10.4 us
    pallas_call x1, Pallas kernels, per_device(): pl.pallas_call(functools.partial(main_kernel, scale, books), out_shape=(j...  8.37 us
  transfers between devices with their start and end apart: 1, of which 1 were waited for; matrix products, arithmetic and copies ran while one was open for 0% of the time, Pallas kernels for 0%

profile of v5, /device:TPU:1, one launch (start us, length us, event | category | flops | bytes accessed | tf_op | source)
XLA Modules:
  0.0 93.0 jit_solution(14506245078364297578)
XLA Ops:
  0.6 1.7 %pack.1 = bf16[16,176,128]{2,1,0:T(8,128)(2,1)} custom-call(bf16[16,768]{1,0:T(8,128)(2,1)} %queries_ref.1, s32[64,128]{1,0:T(8,128)} %bitcast.17, f32[1,16]{1,0:T(1,128)} %bitcast.18, s32[1,16]{1,0:T(1,128)} %bitcast.19), custom_call_target="tpu_custom_call" | custom-call | tf_op jit(solution)/shard_map/pack/pallas_call | solution.py:241
  2.3 0.0 copy-start
  2.3 10.4 %all-to-all-start = ((bf16[16,176,128]{2,1,0:T(8,128)(2,1)}), bf16[16,176,128]{2,1,0:T(8,128)(2,1)S(1)}, u32[]{:S(2)}, u32[]{:S(2)}) async-start(bf16[16,176,128]{2,1,0:T(8,128)(2,1)} %pack.1), calls=%async_computation | async-start | bytes 1441792 | tf_op jit(solution)/shard_map/all_to_all | solution.py:246
  12.7 13.6 %all-to-all-done.group_ref = bf16[16,176,128]{2,1,0:T(8,128)(2,1)S(1)} async-done(((bf16[16,176,128]{2,1,0:T(8,128)(2,1)}), bf16[16,176,128]{2,1,0:T(8,128)(2,1)S(1)}, u32[]{:S(2)}, u32[]{:S(2)}) %all-to-all-start) | async-done | bytes 720928 | tf_op jit(solution)/shard_map/all_to_all | solution.py:246
  26.3 0.0 copy-done
  26.3 8.4 %core.1 = (f32[1,16]{1,0:T(1,128)}, f32[16,768]{1,0:T(8,128)}, bf16[2,768,128]{2,1,0:T(8,128)(2,1)S(1)}) custom-call(s32[1,1]{1,0:T(1,128)} %bitcast.me_ref, bf16[16,176,128]{2,1,0:T(8,128)(2,1)S(1)} %all-to-all-done.group_ref, bf16[768,256]{1,0:T(8,128)(2,1)S(1)} %bitcast.15), custom_call_target="tpu_custom_call" | custom-call | tf_op jit(solution)/shard_map/core/pallas_call | solution.py:248
  34.7 15.7 %all_to_all.20 = bf16[64,24,128]{2,1,0:T(8,128)(2,1)S(1)} all-to-all(bf16[64,24,128]{2,1,0:T(8,128)(2,1)S(1)} %bitcast.14), channel_id=1, replica_groups=mesh['db'=16,'near'=2,'far'=8,'pair'=2] {'db','near','pair'}, dimensions={0} | all-to-all | bytes 786432 | tf_op jit(solution)/shard_map/all_to_all | solution.py:272
  50.4 0.1 reduce_sum.24
  50.5 24.6 %all_to_all.21 = bf16[8,24,128]{2,1,0:T(8,128)(2,1)S(1)} all-to-all(bf16[8,24,128]{2,1,0:T(8,128)(2,1)S(1)} %broadcast_in_dim.4), channel_id=1, replica_groups=mesh['db'=16,'near'=2,'far'=8,'pair'=2] {'far'}, dimensions={0} | all-to-all | bytes 98304 | tf_op jit(solution)/shard_map/all_to_all | solution.py:230
  75.1 0.1 broadcast_in_dim.5
  75.1 16.9 %all_to_all.22 = bf16[64,24,128]{2,1,0:T(8,128)(2,1)S(1)} all-to-all(bf16[64,24,128]{2,1,0:T(8,128)(2,1)S(1)} %broadcast_in_dim.5), channel_id=1, replica_groups=mesh['db'=16,'near'=2,'far'=8,'pair'=2] {'db','near','pair'}, dimensions={0} | all-to-all | bytes 786432 | tf_op jit(solution)/shard_map/all_to_all | solution.py:230
  92.0 0.9 %widen.1 = f32[768,256]{1,0:T(8,128)} custom-call(bf16[2,768,128]{2,1,0:T(8,128)(2,1)S(1)} %bitcast.13), custom_call_target="tpu_custom_call" | custom-call | tf_op jit(solution)/shard_map/widen/pallas_call | solution.py:277
  (2 shorter events, 0.0 us)
Async XLA Ops:
  2.3 24.0 %copy-start = (bf16[64,12,256]{2,0,1:T(8,128)(2,1)S(1)}, bf16[64,12,256]{2,0,1:T(8,128)(2,1)}, u32[]{:S(2)}) copy-start(bf16[64,12,256]{2,0,1:T(8,128)(2,1)} %param.7) | copy-start | bytes 1179652
  2.3 24.0 %all-to-all-start = ((bf16[16,176,128]{2,1,0:T(8,128)(2,1)}), bf16[16,176,128]{2,1,0:T(8,128)(2,1)S(1)}, u32[]{:S(2)}, u32[]{:S(2)}) async-start(bf16[16,176,128]{2,1,0:T(8,128)(2,1)} %pack.1), calls=%async_computation | async-start | bytes 1441792 | tf_op jit(solution)/shard_map/all_to_all | solution.py:246

commit v6 on v5

--- a/solution.py
+++ b/solution.py
@@ -27,6 +27,9 @@
     rows, width = queries_ref.shape
     books = codes_ref.shape[0]
     top = rows * (width // LANES)
+    sorted_rows = jnp.dot(
+        queries_ref[...], order_table(width, books), preferred_element_type=jnp.float32
+    ).astype(jnp.bfloat16)
     code_rows = codes_ref[...].astype(jnp.float32).astype(jnp.bfloat16)
     spot = lax.broadcasted_iota(jnp.int32, (rows, rows), 0)
     lane = lax.broadcasted_iota(jnp.int32, (rows, rows), 1)
@@ -49,9 +52,7 @@
     extra = extra.astype(jnp.bfloat16)
     for d in range(out_ref.shape[0]):
         for j in range(width // LANES):
-            out_ref[d, rows * j : rows * (j + 1), :] = queries_ref[
-                :, LANES * j : LANES * (j + 1)
-            ]
+            out_ref[d, rows * j : rows * (j + 1), :] = sorted_rows[:, LANES * j : LANES * (j + 1)]
         out_ref[d, top : top + books, :] = code_rows
         out_ref[d, top + books :, :] = extra
 
@@ -59,7 +60,7 @@
 def main_kernel(
     scale, books, me_ref, group_ref, cb_ref,
     loss_ref, gq_ref, gb_ref,
-    cb_scr, q_scr, table_scr, sorted_scr, dec_scr, s_scr, max_scr, sum_scr, total_scr, pg_scr,
+    cb_scr, sorted_scr, dec_scr, s_scr, max_scr, sum_scr, total_scr, pg_scr,
 ):
     members = group_ref.shape[0]
     width, levels = cb_ref.shape
@@ -71,13 +72,10 @@
     me = me_ref[0, 0]
     cb_scr[...] = cb_ref[...].astype(jnp.float32)
     for j in range(blocks):
-        q_scr[:, LANES * j : LANES * (j + 1)] = group_ref[
+        sorted_scr[:, LANES * j : LANES * (j + 1)] = group_ref[
             :, rows * j : rows * (j + 1), :
         ].reshape(queries, LANES)
-    table_scr[...] = order_table(width, books)
-    sorted_scr[...] = jnp.dot(
-        q_scr[...], table_scr[...], preferred_element_type=jnp.float32
-    ).astype(jnp.bfloat16)
+    done = []
 
     def decode(t):
         for side in range(2):
@@ -90,6 +88,8 @@
                 index = codes[8 * g : 8 * g + 8, :]
                 inner = index & (LANES - 1)
                 upper = index >= LANES
+                if len(done) >= 4:
+                    inner = inner + (done[-4] * 0.0).astype(jnp.int32)
                 for two in range(sub_width // 2):
                     tiles = []
                     for c in (2 * two, 2 * two + 1):
@@ -97,6 +97,8 @@
                         low = jnp.take_along_axis(cb_scr[at : at + 8, :LANES], inner, axis=1)
                         high = jnp.take_along_axis(cb_scr[at : at + 8, LANES:], inner, axis=1)
                         tiles.append(jnp.where(upper, high, low))
+                    if two == 0:
+                        done.append(tiles[0])
                     at = 8 * sub_width * g + 16 * two
                     dec_scr[t, at : at + 16, LANES * side : LANES * side + LANES] = (
                         jnp.concatenate(tiles, axis=0).astype(jnp.bfloat16)
@@ -210,7 +212,7 @@
     third = grad - first - second
     restored = lax.dot_general(
         jnp.concatenate([first, second, third], axis=0).astype(jnp.bfloat16),
-        table_scr[...],
+        order_table(width, books),
         (((1,), (1,)), ((), ())),
         preferred_element_type=jnp.float32,
     )
@@ -257,8 +259,6 @@
         scratch_shapes=[
             pltpu.VMEM((width, levels), jnp.float32),
             pltpu.VMEM((members * rows, width), jnp.bfloat16),
-            pltpu.VMEM((width, width), jnp.bfloat16),
-            pltpu.VMEM((members * rows, width), jnp.bfloat16),
             pltpu.VMEM((members // 2, width, 2 * LANES), jnp.bfloat16),
             pltpu.VMEM((members, members * rows, LANES), jnp.float32),
             pltpu.VMEM((members * rows, LANES), jnp.float32),

time: 93.3 us -> 93.2 us (level)
  no operation moved by 1% of the time
where the time goes in v6:
time: 93.2 us; the launch traced here: 92.8 us
  blocking collectives  57.2 us (61%)
  waiting for transfers between devices  13.6 us (15%)
  Pallas kernels  10.9 us (12%)
  starting transfers between devices  10.4 us (11%)
    all_to_all x2, blocking collectives, spread(): return lax.all_to_all(copies, axis, 0, 0)  41.4 us
    all_to_all x1, blocking collectives, per_device(): part = lax.all_to_all(book_part.reshape(plane, -1, LANES), PLANE, 0, 0)  15.7 us
    all_to_all x1, waiting for transfers between devices, per_device(): group = lax.all_to_all(pack, 'db', 0, 0)  13.6 us
    all_to_all x1, starting transfers between devices, per_device(): group = lax.all_to_all(pack, 'db', 0, 0)  10.4 us
    pallas_call x1, Pallas kernels, per_device(): pl.pallas_call(functools.partial(main_kernel, scale, books), out_shape=(j...  7.99 us
    pallas_call x1, Pallas kernels, per_device(): pl.pallas_call(pack_kernel, out_shape=jax.ShapeDtypeStruct((members, pack...  1.97 us
  transfers between devices with their start and end apart: 1, of which 1 were waited for; matrix products, arithmetic and copies ran while one was open for 0% of the time, Pallas kernels for 0%

profile of v6, /device:TPU:1, one launch (start us, length us, event | category | flops | bytes accessed | tf_op | source)
XLA Modules:
  0.0 92.8 jit_solution(6292058769346002965)
XLA Ops:
  0.6 2.0 %pack.1 = bf16[16,176,128]{2,1,0:T(8,128)(2,1)} custom-call(bf16[16,768]{1,0:T(8,128)(2,1)} %queries_ref.1, s32[64,128]{1,0:T(8,128)} %bitcast.17, f32[1,16]{1,0:T(1,128)} %bitcast.18, s32[1,16]{1,0:T(1,128)} %bitcast.19), custom_call_target="tpu_custom_call" | custom-call | tf_op jit(solution)/shard_map/pack/pallas_call | solution.py:243
  2.6 0.0 copy-start
  2.6 10.4 %all-to-all-start = ((bf16[16,176,128]{2,1,0:T(8,128)(2,1)}), bf16[16,176,128]{2,1,0:T(8,128)(2,1)S(1)}, u32[]{:S(2)}, u32[]{:S(2)}) async-start(bf16[16,176,128]{2,1,0:T(8,128)(2,1)} %pack.1), calls=%async_computation | async-start | bytes 1441792 | tf_op jit(solution)/shard_map/all_to_all | solution.py:248
  13.0 13.6 %all-to-all-done.group_ref = bf16[16,176,128]{2,1,0:T(8,128)(2,1)S(1)} async-done(((bf16[16,176,128]{2,1,0:T(8,128)(2,1)}), bf16[16,176,128]{2,1,0:T(8,128)(2,1)S(1)}, u32[]{:S(2)}, u32[]{:S(2)}) %all-to-all-start) | async-done | bytes 720928 | tf_op jit(solution)/shard_map/all_to_all | solution.py:248
  26.6 0.0 copy-done
  26.6 8.0 %core.1 = (f32[1,16]{1,0:T(1,128)}, f32[16,768]{1,0:T(8,128)}, bf16[2,768,128]{2,1,0:T(8,128)(2,1)S(1)}) custom-call(s32[1,1]{1,0:T(1,128)} %bitcast.me_ref, bf16[16,176,128]{2,1,0:T(8,128)(2,1)S(1)} %all-to-all-done.group_ref, bf16[768,256]{1,0:T(8,128)(2,1)S(1)} %bitcast.15), custom_call_target="tpu_custom_call" | custom-call | tf_op jit(solution)/shard_map/core/pallas_call | solution.py:250
  34.5 15.7 %all_to_all.20 = bf16[64,24,128]{2,1,0:T(8,128)(2,1)S(1)} all-to-all(bf16[64,24,128]{2,1,0:T(8,128)(2,1)S(1)} %bitcast.14), channel_id=1, replica_groups=mesh['db'=16,'near'=2,'far'=8,'pair'=2] {'db','near','pair'}, dimensions={0} | all-to-all | bytes 786432 | tf_op jit(solution)/shard_map/all_to_all | solution.py:272
  50.3 0.1 reduce_sum.24
  50.4 24.6 %all_to_all.21 = bf16[8,24,128]{2,1,0:T(8,128)(2,1)S(1)} all-to-all(bf16[8,24,128]{2,1,0:T(8,128)(2,1)S(1)} %broadcast_in_dim.4), channel_id=1, replica_groups=mesh['db'=16,'near'=2,'far'=8,'pair'=2] {'far'}, dimensions={0} | all-to-all | bytes 98304 | tf_op jit(solution)/shard_map/all_to_all | solution.py:232
  74.9 0.1 broadcast_in_dim.5
  75.0 16.9 %all_to_all.22 = bf16[64,24,128]{2,1,0:T(8,128)(2,1)S(1)} all-to-all(bf16[64,24,128]{2,1,0:T(8,128)(2,1)S(1)} %broadcast_in_dim.5), channel_id=1, replica_groups=mesh['db'=16,'near'=2,'far'=8,'pair'=2] {'db','near','pair'}, dimensions={0} | all-to-all | bytes 786432 | tf_op jit(solution)/shard_map/all_to_all | solution.py:232
  91.9 0.9 %widen.1 = f32[768,256]{1,0:T(8,128)} custom-call(bf16[2,768,128]{2,1,0:T(8,128)(2,1)S(1)} %bitcast.13), custom_call_target="tpu_custom_call" | custom-call | tf_op jit(solution)/shard_map/widen/pallas_call | solution.py:277
  (2 shorter events, 0.0 us)
Async XLA Ops:
  2.6 24.0 %copy-start = (bf16[64,12,256]{2,0,1:T(8,128)(2,1)S(1)}, bf16[64,12,256]{2,0,1:T(8,128)(2,1)}, u32[]{:S(2)}) copy-start(bf16[64,12,256]{2,0,1:T(8,128)(2,1)} %param.7) | copy-start | bytes 1179652
  2.6 24.0 %all-to-all-start = ((bf16[16,176,128]{2,1,0:T(8,128)(2,1)}), bf16[16,176,128]{2,1,0:T(8,128)(2,1)S(1)}, u32[]{:S(2)}, u32[]{:S(2)}) async-start(bf16[16,176,128]{2,1,0:T(8,128)(2,1)} %pack.1), calls=%async_computation | async-start | bytes 1441792 | tf_op jit(solution)/shard_map/all_to_all | solution.py:248

commit v7 on v4

--- a/solution.py
+++ b/solution.py
@@ -14,15 +14,13 @@
 WHOLE = ("db", "near", "far", "pair")
 
 
-def order_table(width, books, inverse):
+def order_table(width, books, start, count, kind):
     sub_width = width // books
-    row = lax.broadcasted_iota(jnp.int32, (width, 1 if inverse else width), 0)
-    column = lax.broadcasted_iota(jnp.int32, (width if inverse else 1, width), 1)
-    place = row if inverse else column
+    row = lax.broadcasted_iota(jnp.int32, (width, count), 0).astype(kind)
+    place = lax.broadcasted_iota(jnp.int32, (1, count), 1) + start
     inner = place % (8 * sub_width)
     source = (place // (8 * sub_width) * 8 + inner % 8) * sub_width + inner // 8
-    other = column if inverse else row
-    return jnp.where(other == source, 1.0, 0.0).astype(jnp.bfloat16)
+    return jnp.where(row == source.astype(kind), 1.0, 0.0).astype(jnp.bfloat16)
 
 
 def pack_kernel(queries_ref, codes_ref, weight_ref, positive_ref, out_ref):
@@ -76,9 +74,14 @@
         q_scr[:, LANES * j : LANES * (j + 1)] = group_ref[
             :, rows * j : rows * (j + 1), :
         ].reshape(queries, LANES)
-    sorted_scr[...] = jnp.dot(
-        q_scr[...], order_table(width, books, False), preferred_element_type=jnp.float32
-    ).astype(jnp.bfloat16)
+    span = 2 * LANES
+    for j in range(0, width, span):
+        sorted_scr[:, j : j + span] = jnp.dot(
+            q_scr[...],
+            order_table(width, books, j, span, jnp.int32),
+            preferred_element_type=jnp.float32,
+        ).astype(jnp.bfloat16)
+    done = []
 
     def decode(t):
         for side in range(2):
@@ -91,6 +94,8 @@
                 index = codes[8 * g : 8 * g + 8, :]
                 inner = index & (LANES - 1)
                 upper = index >= LANES
+                if len(done) >= 4:
+                    inner = inner + (done[-4] * 0.0).astype(jnp.int32)
                 for two in range(sub_width // 2):
                     tiles = []
                     for c in (2 * two, 2 * two + 1):
@@ -98,6 +103,8 @@
                         low = jnp.take_along_axis(cb_scr[at : at + 8, :LANES], inner, axis=1)
                         high = jnp.take_along_axis(cb_scr[at : at + 8, LANES:], inner, axis=1)
                         tiles.append(jnp.where(upper, high, low))
+                    if two == 0:
+                        done.append(tiles[0])
                     at = 8 * sub_width * g + 16 * two
                     dec_scr[t, at : at + 16, LANES * side : LANES * side + LANES] = (
                         jnp.concatenate(tiles, axis=0).astype(jnp.bfloat16)
@@ -169,18 +176,15 @@
                 )
             )
         terms = pg_scr[sub_width * m : sub_width * m + pair_rows, :]
-        high = terms.astype(jnp.bfloat16).astype(jnp.float32)
-        parts = [
-            jnp.concatenate([jnp.where(upper, x, 0.0), jnp.where(upper, 0.0, x)], axis=1)
-            for x in (high, terms - high)
-        ]
         sums = lax.dot_general(
-            jnp.concatenate(parts, axis=0).astype(jnp.bfloat16),
+            jnp.concatenate(
+                [jnp.where(upper, terms, 0.0), jnp.where(upper, 0.0, terms)], axis=1
+            ).astype(jnp.bfloat16),
             jnp.concatenate(tables, axis=1),
             (((1,), (1,)), ((), ())),
             preferred_element_type=jnp.float32,
         )
-        ready.append(sums[:pair_rows] + sums[pair_rows:])
+        ready.append(sums)
         if m % 4 == 2:
             at = sub_width * (m - 2)
             both = jnp.concatenate(ready, axis=0).astype(jnp.bfloat16)
@@ -209,24 +213,34 @@
             (((1,), (1,)), ((), ())),
             preferred_element_type=jnp.float32,
         )
-    gq_ref[...] = grad
+    first = grad.astype(jnp.bfloat16).astype(jnp.float32)
+    second = (grad - first).astype(jnp.bfloat16).astype(jnp.float32)
+    third = grad - first - second
+    parts = jnp.concatenate([first, second, third], axis=0).astype(jnp.bfloat16)
+    restored = jnp.zeros((3 * rows, width), jnp.float32)
+    for j in range(0, width, span):
+        restored = restored + lax.dot_general(
+            parts[:, j : j + span],
+            order_table(width, books, j, span, jnp.float32),
+            (((1,), (1,)), ((), ())),
+            preferred_element_type=jnp.float32,
+        )
+    gq_ref[...] = restored[:rows] + restored[rows : 2 * rows] + restored[2 * rows :]
     loss = weight * (own_total - jnp.sum(chosen, axis=1, keepdims=True))
     diagonal = lax.broadcasted_iota(jnp.int32, (rows, LANES), 0).astype(jnp.float32) == own_lane
     loss_ref[...] = jnp.sum(jnp.where(diagonal, loss, 0.0), axis=0, keepdims=True)[:, :rows]
 
 
-def restore_kernel(books, grad_ref, out_ref):
-    rows, width = grad_ref.shape
-    grad = grad_ref[...]
-    first = grad.astype(jnp.bfloat16).astype(jnp.float32)
-    second = (grad - first).astype(jnp.bfloat16).astype(jnp.float32)
-    third = grad - first - second
-    restored = jnp.dot(
-        jnp.concatenate([first, second, third], axis=0).astype(jnp.bfloat16),
-        order_table(width, books, True),
-        preferred_element_type=jnp.float32,
-    )
-    out_ref[...] = restored[:rows] + restored[rows : 2 * rows] + restored[2 * rows :]
+def widen_kernel(sub_width, part_ref, out_ref):
+    halves, width, _ = part_ref.shape
+    books = width // sub_width
+    start = lax.broadcasted_iota(jnp.int32, (books, 1), 0) * sub_width
+    column = lax.broadcasted_iota(jnp.int32, (books, width), 1)
+    table = jnp.concatenate(
+        [jnp.where(column - c == start, 1.0, 0.0) for c in range(sub_width)], axis=0
+    ).astype(jnp.bfloat16)
+    part = jnp.concatenate([part_ref[j] for j in range(halves)], axis=1)
+    out_ref[...] = jnp.dot(table, part, preferred_element_type=jnp.float32)
 
 
 def spread(block, axis):
@@ -245,7 +259,6 @@
     pack = pl.pallas_call(
         pack_kernel,
         out_shape=jax.ShapeDtypeStruct((members, pack_rows, LANES), jnp.bfloat16),
-        compiler_params=pltpu.CompilerParams(vmem_limit_bytes=8 * 1024 * 1024),
         name="pack",
     )(queries, passage_codes.T, loss_weight.reshape(1, rows), positives.reshape(1, rows))
     group = lax.all_to_all(pack, "db", 0, 0)
@@ -273,19 +286,19 @@
         compiler_params=pltpu.CompilerParams(vmem_limit_bytes=24 * 1024 * 1024),
         name="core",
     )(me, group, codebooks.transpose(1, 0, 2).reshape(width, levels))
-    grad_queries = pl.pallas_call(
-        functools.partial(restore_kernel, books),
-        out_shape=jax.ShapeDtypeStruct((rows, width), jnp.float32),
-        compiler_params=pltpu.CompilerParams(vmem_limit_bytes=8 * 1024 * 1024),
-        name="restore",
-    )(grad_queries)
     part = lax.all_to_all(book_part.reshape(plane, -1, LANES), PLANE, 0, 0)
     part = jnp.sum(part.astype(jnp.float32), axis=0).astype(jnp.bfloat16)
     part = spread(part, "far")
     part = jnp.sum(part.astype(jnp.float32), axis=0).astype(jnp.bfloat16)
-    part = spread(part, PLANE).astype(jnp.float32)
-    book_total = part.reshape(-1, books, sub_width, LANES).transpose(1, 2, 0, 3)
-    return loss.reshape(rows), grad_queries, book_total.reshape(books, sub_width, levels)
+    part = spread(part, PLANE).reshape(-1, width, LANES)
+    book_total = pl.pallas_call(
+        functools.partial(widen_kernel, sub_width),
+        out_shape=jax.ShapeDtypeStruct((width, levels), jnp.float32),
+        compiler_params=pltpu.CompilerParams(vmem_limit_bytes=8 * 1024 * 1024),
+        name="widen",
+    )(part)
+    book_total = book_total.reshape(sub_width, books, levels).transpose(1, 0, 2)
+    return loss.reshape(rows), grad_queries, book_total
 
 
 def solution(mesh):

time: 95.7 us -> 92.8 us (0.970)
  blocking collectives: 40.3 us -> 57.2 us
  waiting for transfers between devices: 23.6 us -> 13.6 us
  starting transfers between devices: 16.4 us -> 10.4 us
  local copies, waits for them, and re-layouts: 5.15 us -> 0.07 us
  Pallas kernels: 8.95 us -> 10.5 us
    all_to_all x1 -> x2, blocking collectives: 24.6 us -> 41.4 us  [spread(): return lax.all_to_all(copies, axis, 0, 0)]
    all_to_all x1 -> x0, waiting for transfers between devices: 10 us -> none  [spread(): return lax.all_to_all(copies, axis, 0, 0)]
    all_to_all x1 -> x0, starting transfers between devices: 6.03 us -> none  [spread(): return lax.all_to_all(copies, axis, 0, 0)]
    reshape x3 -> x0, local copies, waits for them, and re-layouts: 2.19 us -> none  [per_device(): book_total.reshape(books, sub_width, levels)]
    unnamed x10 -> x2, local copies, waits for them, and re-layouts: 2.15 us -> 0.01 us
  transfers between devices with their start and end apart: 2 -> 1, of which waited for: 2 -> 1; matrix products, arithmetic and copies ran while one was open for 0% -> 0% of each run, Pallas kernels for 1% -> 0%
where the time goes in v7:
time: 92.8 us; the launch traced here: 92.4 us
  blocking collectives  57.2 us (62%)
  waiting for transfers between devices  13.6 us (15%)
  Pallas kernels  10.5 us (11%)
  starting transfers between devices  10.4 us (11%)
    all_to_all x2, blocking collectives, spread(): return lax.all_to_all(copies, axis, 0, 0)  41.4 us
    all_to_all x1, blocking collectives, per_device(): part = lax.all_to_all(book_part.reshape(plane, -1, LANES), PLANE, 0, 0)  15.7 us
    all_to_all x1, waiting for transfers between devices, per_device(): group = lax.all_to_all(pack, 'db', 0, 0)  13.6 us
    all_to_all x1, starting transfers between devices, per_device(): group = lax.all_to_all(pack, 'db', 0, 0)  10.4 us
    pallas_call x1, Pallas kernels, per_device(): pl.pallas_call(functools.partial(main_kernel, scale, books), out_shape=(j...  7.39 us
  transfers between devices with their start and end apart: 1, of which 1 were waited for; matrix products, arithmetic and copies ran while one was open for 0% of the time, Pallas kernels for 0%

profile of v7, /device:TPU:1, one launch (start us, length us, event | category | flops | bytes accessed | tf_op | source)
XLA Modules:
  0.0 92.4 jit_solution(6053536021440192462)
XLA Ops:
  0.6 1.7 %pack.1 = bf16[16,176,128]{2,1,0:T(8,128)(2,1)} custom-call(bf16[16,768]{1,0:T(8,128)(2,1)} %queries_ref.1, s32[64,128]{1,0:T(8,128)} %bitcast.17, f32[1,16]{1,0:T(1,128)} %bitcast.18, s32[1,16]{1,0:T(1,128)} %bitcast.19), custom_call_target="tpu_custom_call" | custom-call | tf_op jit(solution)/shard_map/pack/pallas_call | solution.py:259
  2.3 0.0 copy-start
  2.3 10.4 %all-to-all-start = ((bf16[16,176,128]{2,1,0:T(8,128)(2,1)}), bf16[16,176,128]{2,1,0:T(8,128)(2,1)S(1)}, u32[]{:S(2)}, u32[]{:S(2)}) async-start(bf16[16,176,128]{2,1,0:T(8,128)(2,1)} %pack.1), calls=%async_computation | async-start | bytes 1441792 | tf_op jit(solution)/shard_map/all_to_all | solution.py:264
  12.7 13.6 %all-to-all-done.group_ref = bf16[16,176,128]{2,1,0:T(8,128)(2,1)S(1)} async-done(((bf16[16,176,128]{2,1,0:T(8,128)(2,1)}), bf16[16,176,128]{2,1,0:T(8,128)(2,1)S(1)}, u32[]{:S(2)}, u32[]{:S(2)}) %all-to-all-start) | async-done | bytes 720928 | tf_op jit(solution)/shard_map/all_to_all | solution.py:264
  26.3 0.0 copy-done
  26.3 7.4 %core.1 = (f32[1,16]{1,0:T(1,128)}, f32[16,768]{1,0:T(8,128)}, bf16[2,768,128]{2,1,0:T(8,128)(2,1)S(1)}) custom-call(s32[1,1]{1,0:T(1,128)} %bitcast.me_ref, bf16[16,176,128]{2,1,0:T(8,128)(2,1)S(1)} %all-to-all-done.group_ref, bf16[768,256]{1,0:T(8,128)(2,1)S(1)} %bitcast.15), custom_call_target="tpu_custom_call" | custom-call | tf_op jit(solution)/shard_map/core/pallas_call | solution.py:266
  33.7 15.7 %all_to_all.20 = bf16[64,24,128]{2,1,0:T(8,128)(2,1)S(1)} all-to-all(bf16[64,24,128]{2,1,0:T(8,128)(2,1)S(1)} %bitcast.14), channel_id=1, replica_groups=mesh['db'=16,'near'=2,'far'=8,'pair'=2] {'db','near','pair'}, dimensions={0} | all-to-all | bytes 786432 | tf_op jit(solution)/shard_map/all_to_all | solution.py:289
  49.4 0.1 reduce_sum.24
  49.5 24.6 %all_to_all.21 = bf16[8,24,128]{2,1,0:T(8,128)(2,1)S(1)} all-to-all(bf16[8,24,128]{2,1,0:T(8,128)(2,1)S(1)} %broadcast_in_dim.4), channel_id=1, replica_groups=mesh['db'=16,'near'=2,'far'=8,'pair'=2] {'far'}, dimensions={0} | all-to-all | bytes 98304 | tf_op jit(solution)/shard_map/all_to_all | solution.py:248
  74.1 0.1 broadcast_in_dim.5
  74.1 16.9 %all_to_all.22 = bf16[64,24,128]{2,1,0:T(8,128)(2,1)S(1)} all-to-all(bf16[64,24,128]{2,1,0:T(8,128)(2,1)S(1)} %broadcast_in_dim.5), channel_id=1, replica_groups=mesh['db'=16,'near'=2,'far'=8,'pair'=2] {'db','near','pair'}, dimensions={0} | all-to-all | bytes 786432 | tf_op jit(solution)/shard_map/all_to_all | solution.py:248
  91.0 1.4 %widen.1 = f32[768,256]{1,0:T(8,128)} custom-call(bf16[2,768,128]{2,1,0:T(8,128)(2,1)S(1)} %bitcast.13), custom_call_target="tpu_custom_call" | custom-call | tf_op jit(solution)/shard_map/widen/pallas_call | solution.py:294
  (2 shorter events, 0.0 us)
Async XLA Ops:
  2.3 24.0 %copy-start = (bf16[64,12,256]{2,0,1:T(8,128)(2,1)S(1)}, bf16[64,12,256]{2,0,1:T(8,128)(2,1)}, u32[]{:S(2)}) copy-start(bf16[64,12,256]{2,0,1:T(8,128)(2,1)} %param.7) | copy-start | bytes 1179652
  2.3 24.0 %all-to-all-start = ((bf16[16,176,128]{2,1,0:T(8,128)(2,1)}), bf16[16,176,128]{2,1,0:T(8,128)(2,1)S(1)}, u32[]{:S(2)}, u32[]{:S(2)}) async-start(bf16[16,176,128]{2,1,0:T(8,128)(2,1)} %pack.1), calls=%async_computation | async-start | bytes 1441792 | tf_op jit(solution)/shard_map/all_to_all | solution.py:264
